TPU v7x, 32 devices: a whole 2x2x4 slice. The times are simulated.
32 devices in a mesh: mat: 4 (over z), pts: 8 (over y, x, core).
Axes of the slice: x: 2, y: 2, z: 4, core: 2. Of those that a mesh axis runs over, the one named last changes fastest.
Arguments:
- basis_values: bfloat16 [128, 2048, 512], P(('mat', 'pts')), may hold values from -6 to 6
- tile_ids: int32 [128, 4], P(('mat', 'pts')), may hold values from 0 to 3, as said below
- density_matrix: bfloat16 [512, 512], P('mat'), may hold values from -0.01171875 to 0.01171875
- descriptors: bfloat16 [128, 2048, 64], P(('mat', 'pts')), may hold values from -6 to 6
- grid_weights: float32 [128, 2048], P(('mat', 'pts')), may hold values from 0.25 to 2
- centre_ids: int32 [128, 2048], P(('mat', 'pts')), may hold values from 0 to 127
- density_scale: float32 [64], replicated, may hold values from -4 to 4
- norm_gain: float32 [64], replicated, may hold values from 0.1 to 1.9
- w_first: bfloat16 [64, 256], replicated, may hold values from -0.75 to 0.75
- b_first: float32 [256], replicated, may hold values from -3 to 3
- w_second: bfloat16 [256, 256], replicated, may hold values from -0.375 to 0.375
- b_second: float32 [256], replicated, may hold values from -3 to 3
- w_third: bfloat16 [256, 64], replicated, may hold values from -0.375 to 0.375
- b_third: float32 [64], replicated, may hold values from -3 to 3
Outputs:
- potential_matrix: bfloat16 [512, 512], P('mat', 'pts')
- centre_features: bfloat16 [128, 64], P('pts')
Inputs may be any that keep to these rules, and one draw needn't show every extreme that they name: `tile_ids`: the 4 tiles t of one batch have 4 different values of t.
All inputs are finite; a program needn't handle non-finite values.
Results may differ from a plain program's by a relative error of at most 0.0064.
Values may be sent and summed in bfloat16 or wider, within the bound.
A program may use at most 64 MiB of HBM per device.

v0:
```python
import functools
import math

import jax
import jax.numpy as jnp
from jax import lax
from jax.experimental import pallas as pl
from jax.experimental.pallas import tpu as pltpu
from jax.sharding import PartitionSpec as P

CHUNK = 512
SPLIT = 2
MESH = pl.DeviceIdType.MESH
F32 = jnp.float32
BF16 = jnp.bfloat16
NT_DIMS = (((1,), (1,)), ((), ()))


def silu(v):
    h = 0.5 * v
    return h + h * jnp.tanh(h)


def place(pot, cf, out_pot, out_cf):
    out_pot[...] = pot[...]
    out_cf[...] = cf[...]


def kernel(
    nm, npts, factor,
    v_hbm, d_hbm, tiles, dm, gw, ids, scale, gain, w1, b1, w2, b2, w3, b3,
    out_pot, out_cf,
    vbuf, dbuf, vt, dt, oh, gws, dens, pps, panel, cpart, cs_src, cs_in, cz_src, cz_in,
    full, cf_s, cft, acc, snd, rin, red, zsnd, zin,
    vsem, dsem, ag_s, ag_r, fw_s, fw_r, cs_s, cs_r, cz_s, cz_r, cg_s, cg_r, rp_s, rp_r, rz_s, rz_r,
):
    m = lax.axis_index("mat")
    p = lax.axis_index("pts")
    batches, points, orbitals = vbuf.shape
    per_batch = tiles.shape[1]
    tile = orbitals // per_batch
    rows, nb = dm.shape
    ntile = nb // tile
    feat = dbuf.shape[1]
    ncent = oh.shape[1]
    per = points // CHUNK
    chunks = batches * per
    slab = nb // npts
    piece = rows // SPLIT

    for b in range(batches):
        pltpu.make_async_copy(v_hbm.at[b], vbuf.at[b], vsem.at[b]).start()
        pltpu.make_async_copy(d_hbm.at[b], dbuf.at[b], dsem.at[b]).start()

    barrier = pltpu.get_barrier_semaphore()
    for k in range(1, npts):
        pl.semaphore_signal(barrier, inc=1, device_id={"pts": lax.rem(p + k, npts)}, device_id_type=MESH)
    for k in range(1, nm):
        pl.semaphore_signal(barrier, inc=1, device_id={"mat": lax.rem(m + k, nm)}, device_id_type=MESH)
    pl.semaphore_wait(barrier, npts + nm - 2)

    def remote(src, dst, s, r, **where):
        return pltpu.make_async_remote_copy(
            src_ref=src, dst_ref=dst, send_sem=s, recv_sem=r, device_id=where, device_id_type=MESH
        )

    def at_rows(owner, part):
        return pl.ds(pl.multiple_of(owner * rows + part * piece, piece), piece)

    g = lax.rem(p, SPLIT)
    base = p - g
    ag = []
    for k in range(1, nm):
        ag.append(remote(
            dm.at[pl.ds(pl.multiple_of(g * piece, piece), piece)], panel.at[at_rows(m, g)],
            ag_s.at[k - 1], ag_r.at[k - 1], mat=lax.rem(m + k, nm)))
    for c in ag:
        c.start()
    panel[pl.ds(pl.multiple_of(m * rows, rows), rows), :] = dm[...]

    def prepare(b):
        pltpu.make_async_copy(v_hbm.at[b], vbuf.at[b], vsem.at[b]).wait()
        pltpu.make_async_copy(d_hbm.at[b], dbuf.at[b], dsem.at[b]).wait()
        held = [tiles[b, j] for j in range(per_batch)]

        def body(i, carry):
            ch = b * per + i
            r0 = pl.multiple_of(i * CHUNK, CHUNK)
            for t in range(ntile):
                x = vbuf[b, pl.ds(r0, CHUNK), 0:tile]
                if ntile != per_batch:
                    x = jnp.where(held[0] == t, x, jnp.zeros_like(x))
                for j in range(1, per_batch):
                    x = jnp.where(held[j] == t, vbuf[b, pl.ds(r0, CHUNK), j * tile:(j + 1) * tile], x)
                x = x.T
                vt[ch, t * tile:(t + 1) * tile, :] = x
            dt[ch] = dbuf[b, :, pl.ds(r0, CHUNK)]
            row = ids[b:b + 1, pl.ds(r0, CHUNK)]
            which = lax.broadcasted_iota(jnp.int32, (ncent, CHUNK), 0)
            oh[ch] = jnp.where(which == row, 1.0, 0.0).astype(BF16)
            gws[ch] = gw[b:b + 1, pl.ds(r0, CHUNK)]
            return carry

        lax.fori_loop(0, per, body, 0)

    fw = []
    for b in range(batches):
        prepare(b)
        if b == min(1, batches - 1):
            for k in range(1, nm):
                ag[k - 1].wait_recv()
                held = panel.at[at_rows(lax.rem(m - k + nm, nm), g)]
                for s in range(1, SPLIT):
                    i = (k - 1) * (SPLIT - 1) + s - 1
                    c = remote(held, held, fw_s.at[i], fw_r.at[i], pts=base + lax.rem(g + s, SPLIT))
                    c.start()
                    fw.append(c)
    for c in fw:
        c.wait_recv()

    scale_col = jnp.broadcast_to(scale[...], (128, feat)).T[:, :1]
    cpart[...] = jnp.zeros_like(cpart)

    def density_step(ch, carry):
        x = vt[ch]
        q = jnp.dot(panel[...], x, preferred_element_type=F32)
        d = jnp.sum(q * x.astype(F32), axis=0, keepdims=True)
        dens[ch] = d
        wf = gws[ch] * silu(d * scale_col + dt[ch].astype(F32))
        high = wf.astype(BF16)
        low = (wf - high.astype(F32)).astype(BF16)
        both = lax.dot_general(
            jnp.concatenate([high, low], axis=0), oh[ch], NT_DIMS, preferred_element_type=F32)
        cpart[...] += both[:feat] + both[feat:]
        return carry

    lax.fori_loop(0, chunks, density_step, 0)

    fp = feat // npts
    for i in range(npts):
        cs_src[i] = cpart[i * fp:(i + 1) * fp, :]
    cs = []
    for k in range(1, npts):
        to = lax.rem(p + k, npts)
        c = remote(cs_src.at[to], cs_in.at[k - 1], cs_s.at[k - 1], cs_r.at[k - 1], pts=to)
        c.start()
        cs.append(c)
    mine = cs_src[p]
    for k in range(1, npts):
        cs[k - 1].wait_recv()
        mine = mine + cs_in[k - 1]
    cz_src[...] = mine
    cz = []
    for k in range(1, nm):
        c = remote(cz_src, cz_in.at[m], cz_s.at[k - 1], cz_r.at[k - 1], mat=lax.rem(m + k, nm))
        c.start()
        cz.append(c)
    cz_in[m] = mine
    for c in cz:
        c.wait_recv()
    total = cz_in[0]
    for i in range(1, nm):
        total = total + cz_in[i]
    full[p] = total
    cg = []
    for k in range(1, npts):
        c = remote(full.at[p], full.at[p], cg_s.at[k - 1], cg_r.at[k - 1], pts=lax.rem(p + k, npts))
        c.start()
        cg.append(c)
    for c in cg:
        c.wait_recv()

    summed = jnp.concatenate([full[i] for i in range(npts)], axis=0).T
    inverse = lax.rsqrt(jnp.mean(summed * summed, axis=1, keepdims=True) + 1e-05)
    normed = (summed * inverse * gain[...]).astype(BF16)
    one = silu(jnp.dot(normed, w1[...], preferred_element_type=F32) + b1[...]).astype(BF16)
    two = silu(jnp.dot(one, w2[...], preferred_element_type=F32) + b2[...]).astype(BF16)
    cf = (lax.dot_general(two, w3[...], NT_DIMS, preferred_element_type=F32) + b3[...]).astype(BF16).astype(F32)
    cf_s[...] = cf
    cft[...] = cf.T.astype(BF16)
    cent = out_cf.shape[0]
    out_cf[...] = cf_s[pl.ds(pl.multiple_of(p * cent, cent), cent), :].astype(BF16)

    half = nb // 2
    hp = npts // 2
    acc[...] = jnp.zeros_like(acc)
    rp = []
    for h in range(2):
        def block_step(ch, carry):
            if h == 0:
                near = jnp.dot(cft[...], oh[ch], preferred_element_type=F32)
                along = jnp.sum(near * dt[ch].astype(F32), axis=0, keepdims=True)
                pp = gws[ch] * dens[ch] * along * factor
                pps[ch] = pp
            else:
                pp = pps[ch]
            w = (vt[ch, h * half:(h + 1) * half, :].astype(F32) * pp).astype(BF16)
            right = vt[ch] if h == 0 else vt[ch, half:, :]
            r = lax.dot_general(w, right, NT_DIMS, preferred_element_type=F32)
            acc[h * hp:(h + 1) * hp, :, h * half:] += r.reshape(hp, slab, nb - h * half)
            return carry

        if h == 1:
            corner = acc[:hp, :, half:].reshape(half, half)
            acc[hp:, :, :half] = corner.T.reshape(hp, slab, half)
        lax.fori_loop(0, chunks, block_step, 0)
        for i in range(h * hp, (h + 1) * hp):
            snd[i] = acc[i].astype(BF16)
        for k in list(range(1, hp)) + [0]:
            to = h * hp + lax.rem(p + k, hp)
            c = remote(snd.at[to], rin.at[p], rp_s.at[to], rp_r.at[p], pts=to)
            rp.append((to, c))

            @pl.when(to != p)
            def _():
                c.start()

    mine = acc[p]
    for k in range(1, npts):
        src = lax.rem(p + k, npts)
        remote(snd.at[src], rin.at[src], rp_s.at[src], rp_r.at[src], pts=src).wait_recv()
        mine = mine + rin[src].astype(F32)
    width = nb // nm
    for j in range(nm):
        red[j] = mine[:, j * width:(j + 1) * width]
        zsnd[j] = mine[:, j * width:(j + 1) * width].astype(BF16)
    rz = []
    for k in range(1, nm):
        to = lax.rem(m + k, nm)
        c = remote(zsnd.at[to], zin.at[k - 1], rz_s.at[k - 1], rz_r.at[k - 1], mat=to)
        c.start()
        rz.append(c)
    mine = red[m]
    for k in range(1, nm):
        rz[k - 1].wait_recv()
        mine = mine + zin[k - 1].astype(F32)
    out_pot[...] = mine.astype(BF16)

    for c in ag + fw + cs + cz + cg + rz:
        c.wait_send()
    for to, c in rp:
        @pl.when(to != p)
        def _():
            c.wait_send()


def shards(
    nm, npts,
    basis_values, tile_ids, density_matrix, descriptors, grid_weights, centre_ids,
    density_scale, norm_gain, w_first, b_first, w_second, b_second, w_third, b_third,
):
    batches, points, orbitals = basis_values.shape
    per_batch = tile_ids.shape[1]
    tile = orbitals // per_batch
    rows, nb = density_matrix.shape
    feat = descriptors.shape[2]
    ntile = nb // tile
    cent = 16
    ncent = cent * npts
    chunks = batches * points // CHUNK
    slab = nb // npts
    width = nb // nm
    factor = ntile / (per_batch * math.sqrt(points * feat * batches * nm * npts))
    vm = pl.BlockSpec(memory_space=pltpu.VMEM)
    anyw = pl.BlockSpec(memory_space=pl.ANY)
    fp = feat // npts
    dma = pltpu.SemaphoreType.DMA
    nfw = (nm - 1) * (SPLIT - 1)
    potential, centre_features = pl.pallas_call(
        functools.partial(kernel, nm, npts, factor),
        out_shape=(
            jax.ShapeDtypeStruct((slab, width), BF16),
            jax.ShapeDtypeStruct((cent, feat), BF16),
        ),
        in_specs=[anyw, anyw, pl.BlockSpec(memory_space=pltpu.SMEM)] + [vm] * 11,
        out_specs=(vm, vm),
        scratch_shapes=[
            pltpu.VMEM((batches, points, orbitals), BF16),
            pltpu.VMEM((batches, feat, points), BF16),
            pltpu.VMEM((chunks, nb, CHUNK), BF16),
            pltpu.VMEM((chunks, feat, CHUNK), BF16),
            pltpu.VMEM((chunks, ncent, CHUNK), BF16),
            pltpu.VMEM((chunks, 1, CHUNK), F32),
            pltpu.VMEM((chunks, 1, CHUNK), F32),
            pltpu.VMEM((chunks, 1, CHUNK), F32),
            pltpu.VMEM((nb, nb), BF16),
            pltpu.VMEM((feat, ncent), F32),
            pltpu.VMEM((npts, fp, ncent), F32),
            pltpu.VMEM((npts, fp, ncent), F32),
            pltpu.VMEM((fp, ncent), F32),
            pltpu.VMEM((nm, fp, ncent), F32),
            pltpu.VMEM((npts, fp, ncent), F32),
            pltpu.VMEM((ncent, feat), F32),
            pltpu.VMEM((feat, ncent), BF16),
            pltpu.VMEM((npts, slab, nb), F32),
            pltpu.VMEM((npts, slab, nb), BF16),
            pltpu.VMEM((npts, slab, nb), BF16),
            pltpu.VMEM((nm, slab, width), F32),
            pltpu.VMEM((nm, slab, width), BF16),
            pltpu.VMEM((nm, slab, width), BF16),
            dma((batches,)), dma((batches,)),
            dma((nm - 1,)), dma((nm - 1,)),
            dma((nfw,)), dma((nfw,)),
            dma((npts - 1,)), dma((npts - 1,)),
            dma((nm - 1,)), dma((nm - 1,)),
            dma((npts - 1,)), dma((npts - 1,)),
            dma((npts,)), dma((npts,)),
            dma((nm - 1,)), dma((nm - 1,)),
        ],
        compiler_params=pltpu.CompilerParams(
            collective_id=0, has_side_effects=True, vmem_limit_bytes=60 * 1024 * 1024
        ),
    )(
        basis_values, descriptors.transpose(0, 2, 1), tile_ids, density_matrix, grid_weights, centre_ids,
        density_scale.reshape(1, -1), norm_gain.reshape(1, -1),
        w_first, b_first.reshape(1, -1), w_second, b_second.reshape(1, -1),
        w_third.T, b_third.reshape(1, -1),
    )
    potential, centre_features = pl.pallas_call(
        place,
        out_shape=(
            jax.ShapeDtypeStruct((slab, width), BF16),
            jax.ShapeDtypeStruct((cent, feat), BF16),
        ),
        in_specs=[vm, vm],
        out_specs=(vm, vm),
    )(potential, centre_features)
    return (potential.T, centre_features)


def solution(mesh):
    return jax.shard_map(
        functools.partial(shards, mesh.shape["mat"], mesh.shape["pts"]),
        mesh=mesh,
        in_specs=(
            P(("mat", "pts"), None, None),
            P(("mat", "pts"), None),
            P("mat", None),
            P(("mat", "pts"), None, None),
            P(("mat", "pts"), None),
            P(("mat", "pts"), None),
            P(), P(), P(), P(), P(), P(), P(), P(),
        ),
        out_specs=(P("mat", "pts"), P("pts", None)),
        check_vma=False,
    )
```

profile of v0, /device:TPU:4, one launch (start us, length us, event | category | flops | bytes accessed | tf_op | source)
XLA Modules:
  0.0 60.8 jit_solution(12849876950956913234)
XLA Ops:
  0.6 58.8 %shard_map.149 = (bf16[64,128]{1,0:T(8,128)(2,1)}, bf16[16,64]{1,0:T(8,128)(2,1)}) custom-call(bf16[4,2048,512]{2,1,0:T(8,128)(2,1)} %v_hbm.1, bf16[4,64,2048]{2,1,0:T(8,128)(2,1)} %bitcast.8, s32[4,4]{1,0:T(4,128)} %tiles.1, bf16[128,512]{1,0:T(8,128)(2,1)} %dm.1, f32[4,2048]{1,0:T(4,128)} %gw.1, s32[4,2048]{1,0:T(4,128)} %ids.1, f32[1,64]{1,0:T(1,128)} %bitcast.12, ...), custom_call_target="tpu_custom_call" | custom-call | tf_op jit(solution)/shard_map/pallas_call | solution.py:269
  59.5 1.3 %shard_map.150 = (bf16[64,128]{1,0:T(8,128)(2,1)}, bf16[16,64]{1,0:T(8,128)(2,1)}) custom-call(bf16[64,128]{1,0:T(8,128)(2,1)} %get-tuple-element.6.pot, bf16[16,64]{1,0:T(8,128)(2,1)} %get-tuple-element.7.cf), custom_call_target="tpu_custom_call" | custom-call | tf_op jit(solution)/shard_map/pallas_call | solution.py:319
where the time goes:
time: 61 us; the launch traced here: 60.8 us
  Pallas kernels  60.2 us (99%)
  between operations  0.64 us (1%)
    pallas_call x1, Pallas kernels, shards(): pl.pallas_call(functools.partial(kernel, nm, npts, factor), out_shape=(ja...  58.8 us
    pallas_call x1, Pallas kernels, shards(): pl.pallas_call(place, out_shape=(jax.ShapeDtypeStruct((slab, width), BF16...  1.33 us

commit v1 on v0

v1 whole, which is shorter than its diff:
```python
import functools
import math

import jax
import jax.numpy as jnp
from jax import lax
from jax.experimental import pallas as pl
from jax.experimental.pallas import tpu as pltpu
from jax.sharding import PartitionSpec as P

CHUNK = 512
SPLIT = 2
MESH = pl.DeviceIdType.MESH
F32 = jnp.float32
BF16 = jnp.bfloat16
NT_DIMS = (((1,), (1,)), ((), ()))


def silu(v):
    h = 0.5 * v
    return h + h * jnp.tanh(h)


def place(pot, cf, out_pot, out_cf):
    out_pot[...] = pot[...]
    out_cf[...] = cf[...]


def kernel(
    nm, npts, factor,
    v_hbm, d_hbm, tiles_hbm, dm_hbm, gw_hbm, ids_hbm, scale_hbm, gain_hbm,
    w1_hbm, b1_hbm, w2_hbm, b2_hbm, w3_hbm, b3_hbm,
    out_pot, out_cf,
    tiles, dm, gw, ids, scale, gain, w1, b1, w2, b2, w3, b3,
    vbuf, dbuf, vt, oh, dens, pps, panel, cpart, cs_src, cs_in, cz_src, cz_in,
    full, cf_s, cft, acc, snd, rin, red, zsnd, zin,
    isem, vsem, dsem, ag_s, ag_r, fw_s, fw_r, cs_s, cs_r, cz_s, cz_r, cg_s, cg_r, rp_s, rp_r, rz_s, rz_r,
):
    m = lax.axis_index("mat")
    p = lax.axis_index("pts")
    batches = len(vbuf)
    per_batch, points, tile = vbuf[0].shape
    rows, nb = dm.shape
    ntile = nb // tile
    feat = dbuf.shape[1]
    ncent = oh.shape[1]
    per = points // CHUNK
    slab = nb // npts
    piece = rows // SPLIT

    small = [
        pltpu.make_async_copy(a, b, isem.at[i]) for i, (a, b) in enumerate((
            (tiles_hbm, tiles), (dm_hbm, dm), (ids_hbm, ids), (gw_hbm, gw), (scale_hbm, scale), (gain_hbm, gain),
            (w1_hbm, w1), (b1_hbm, b1), (w2_hbm, w2), (b2_hbm, b2), (w3_hbm, w3), (b3_hbm, b3)))]

    def vcopy(b, j):
        return pltpu.make_async_copy(v_hbm.at[b, :, pl.ds(j * tile, tile)], vbuf[b].at[j], vsem.at[b, j])

    def dcopy(b):
        return pltpu.make_async_copy(d_hbm.at[b], dbuf.at[b], dsem.at[b])

    barrier = pltpu.get_barrier_semaphore()
    for k in range(1, npts):
        pl.semaphore_signal(barrier, inc=1, device_id={"pts": lax.rem(p + k, npts)}, device_id_type=MESH)
    for k in range(1, nm):
        pl.semaphore_signal(barrier, inc=1, device_id={"mat": lax.rem(m + k, nm)}, device_id_type=MESH)
    for c in small[:3]:
        c.start()
    for j in range(per_batch):
        vcopy(0, j).start()
    for c in small[3:]:
        c.start()
    for b in range(1, batches):
        for j in range(per_batch):
            vcopy(b, j).start()
    for b in range(batches):
        dcopy(b).start()
    for c in small[:3]:
        c.wait()
    pl.semaphore_wait(barrier, npts + nm - 2)

    def remote(src, dst, s, r, **where):
        return pltpu.make_async_remote_copy(
            src_ref=src, dst_ref=dst, send_sem=s, recv_sem=r, device_id=where, device_id_type=MESH
        )

    def at_rows(owner, part):
        return pl.ds(pl.multiple_of(owner * rows + part * piece, piece), piece)

    g = lax.rem(p, SPLIT)
    base = p - g
    peer = [lax.rem(m + k, nm) for k in range(nm)]
    near = m + 1 - 2 * lax.rem(m, 2)
    order = [near] + [lax.rem(m + 2 * (k // 2) + lax.rem(m + k, 2) - lax.rem(m, 2) + nm, nm) for k in range(2, nm)]
    ag = []
    for k, to in enumerate(order):
        ag.append(remote(
            dm.at[pl.ds(pl.multiple_of(g * piece, piece), piece)], panel.at[at_rows(m, g)],
            ag_s.at[to], ag_r.at[m], mat=to))
    for c in ag:
        c.start()
    panel[pl.ds(pl.multiple_of(m * rows, rows), rows), :] = dm[...]

    def prepare(b):
        for j in range(per_batch):
            vcopy(b, j).wait()
        held = [tiles[b, j] for j in range(per_batch)]

        def find(t, value, otherwise):
            for j in range(per_batch):
                otherwise = jnp.where(held[j] == t, value(j), otherwise)
            return otherwise

        spot = [find(t, lambda j: j, 0) for t in range(ntile)]
        here = [find(t, lambda j: 1, 0) for t in range(ntile)]

        def body(i, carry):
            at = pl.ds(pl.multiple_of(i * CHUNK, CHUNK), CHUNK)
            for t in range(ntile):
                x = vbuf[b][spot[t], at, :]
                if ntile != per_batch:
                    x = jnp.where(here[t] == 1, x, jnp.zeros_like(x))
                vt[b, t * tile:(t + 1) * tile, at] = x.T
            which = lax.broadcasted_iota(jnp.int32, (ncent, CHUNK), 0)
            oh[b, :, at] = jnp.where(which == ids[b:b + 1, at], 1.0, 0.0).astype(BF16)
            return carry

        lax.fori_loop(0, per, body, 0)

    for b in range(batches):
        prepare(b)
    for c in small[3:]:
        c.wait()

    scale_col = jnp.broadcast_to(scale[...], (128, feat)).T[:, :1]
    cpart[...] = jnp.zeros_like(cpart)

    fw = []

    def receive(k):
        src = order[k]
        remote(dm.at[pl.ds(0, piece)], panel.at[at_rows(src, g)], ag_s.at[src], ag_r.at[src], mat=src).wait_recv()
        held = panel.at[at_rows(src, g)]
        mine = []
        for s in range(1, SPLIT):
            i = k * (SPLIT - 1) + s - 1
            c = remote(held, held, fw_s.at[i], fw_r.at[i], pts=base + lax.rem(g + s, SPLIT))
            c.start()
            mine.append(c)
        fw.extend(mine)
        return mine

    def part(b, pair):
        at = pl.ds(pl.multiple_of(pair * 2 * rows, 2 * rows), 2 * rows)
        q = jnp.dot(panel[at, :], vt[b], preferred_element_type=F32)
        return jnp.sum(q * vt[b, at, :].astype(F32), axis=0, keepdims=True)

    pairs = nm // 2
    own = m // 2
    for c in receive(0):
        c.wait_recv()

    def first(b, carry):
        dens[b] = part(b, own)
        return carry

    lax.fori_loop(0, batches, first, 0)
    for k in range(1, nm - 1):
        receive(k)
    for c in fw[SPLIT - 1:]:
        c.wait_recv()

    def second(b, carry):
        d = dens[b]
        for k in range(1, pairs):
            d = d + part(b, lax.rem(own + k, pairs))
        dens[b] = d
        dcopy(b).wait()
        wf = gw[pl.ds(b, 1), :] * silu(d * scale_col + dbuf[b].astype(F32))
        high = wf.astype(BF16)
        low = (wf - high.astype(F32)).astype(BF16)
        both = lax.dot_general(
            jnp.concatenate([high, low], axis=0), oh[b], NT_DIMS, preferred_element_type=F32)
        cpart[...] += both[:feat] + both[feat:]
        return carry

    lax.fori_loop(0, batches, second, 0)

    fp = feat // npts
    for i in range(npts):
        cs_src[i] = cpart[i * fp:(i + 1) * fp, :]
    cs = []
    for k in range(1, npts):
        to = lax.rem(p + k, npts)
        c = remote(cs_src.at[to], cs_in.at[k - 1], cs_s.at[k - 1], cs_r.at[k - 1], pts=to)
        c.start()
        cs.append(c)
    mine = cs_src[p]
    for k in range(1, npts):
        cs[k - 1].wait_recv()
        mine = mine + cs_in[k - 1]
    cz_src[...] = mine
    cz = []
    for k in range(1, nm):
        c = remote(cz_src, cz_in.at[m], cz_s.at[k - 1], cz_r.at[k - 1], mat=lax.rem(m + k, nm))
        c.start()
        cz.append(c)
    cz_in[m] = mine
    for c in cz:
        c.wait_recv()
    total = cz_in[0]
    for i in range(1, nm):
        total = total + cz_in[i]
    full[p] = total
    cg = []
    for k in range(1, npts):
        c = remote(full.at[p], full.at[p], cg_s.at[k - 1], cg_r.at[k - 1], pts=lax.rem(p + k, npts))
        c.start()
        cg.append(c)
    for c in cg:
        c.wait_recv()

    summed = jnp.concatenate([full[i] for i in range(npts)], axis=0).T
    inverse = lax.rsqrt(jnp.mean(summed * summed, axis=1, keepdims=True) + 1e-05)
    normed = (summed * inverse * gain[...]).astype(BF16)
    one = silu(jnp.dot(normed, w1[...], preferred_element_type=F32) + b1[...]).astype(BF16)
    two = silu(jnp.dot(one, w2[...], preferred_element_type=F32) + b2[...]).astype(BF16)
    cf = (lax.dot_general(two, w3[...], NT_DIMS, preferred_element_type=F32) + b3[...]).astype(BF16).astype(F32)
    cf_s[...] = cf
    cft[...] = cf.T.astype(BF16)
    cent = out_cf.shape[0]
    out_cf[...] = cf_s[pl.ds(pl.multiple_of(p * cent, cent), cent), :].astype(BF16)

    group = [[t for t in range(ntile) if (t + t // 2) % 2 == s] for s in range(2)]
    per_tile = tile // slab
    owners = [[t * per_tile + i for t in group[s] for i in range(per_tile)] for s in range(2)]
    width = nb // nm
    half = nb // 2
    acc[...] = jnp.zeros_like(acc)

    def side(b, s):
        return jnp.concatenate([vt[b, t * tile:(t + 1) * tile, :] for t in group[s]], axis=0)

    def block0(b, carry):
        nearest = jnp.dot(cft[...], oh[b], preferred_element_type=F32)
        along = jnp.sum(nearest * dbuf[b].astype(F32), axis=0, keepdims=True)
        pp = gw[pl.ds(b, 1), :] * dens[b] * along * factor
        pps[b] = pp
        w = (side(b, 0).astype(F32) * pp).astype(BF16)
        r = lax.dot_general(w, side(b, 0), NT_DIMS, preferred_element_type=F32)
        for i, o in enumerate(owners[0]):
            acc[o, 0] += r[i * slab:(i + 1) * slab]
        r = lax.dot_general(w, side(b, 1), NT_DIMS, preferred_element_type=F32)
        for i, o in enumerate(owners[0]):
            acc[o, 1] += r[i * slab:(i + 1) * slab]
        return carry

    def block1(b, carry):
        x = side(b, 1)
        w = (x.astype(F32) * pps[b]).astype(BF16)
        r = lax.dot_general(w, x, NT_DIMS, preferred_element_type=F32)
        for i, o in enumerate(owners[1]):
            acc[o, 1] += r[i * slab:(i + 1) * slab]
        return carry

    def send(to, s):
        c = remote(snd.at[to, s], rin.at[p, s], rp_s.at[to, s], rp_r.at[p, s], pts=to)

        @pl.when(to != p)
        def _():
            c.start()

    lax.fori_loop(0, batches, block0, 0)
    for o in owners[0]:
        snd[o, 0] = acc[o, 0].astype(BF16)
        snd[o, 1] = acc[o, 1].astype(BF16)
    across = jnp.concatenate([acc[o, 1] for o in owners[0]], axis=0).T
    for i, o in enumerate(owners[1]):
        acc[o, 0] = across[i * slab:(i + 1) * slab]
        snd[o, 0] = across[i * slab:(i + 1) * slab].astype(BF16)
    for o in range(npts):
        send(o, 0)
        if o in owners[0]:
            send(o, 1)
    lax.fori_loop(0, batches, block1, 0)
    for o in owners[1]:
        snd[o, 1] = acc[o, 1].astype(BF16)
        send(o, 1)
    for s in range(2):
        mine = acc[p, s]
        for k in range(1, npts):
            src = lax.rem(p + k, npts)
            remote(snd.at[src, s], rin.at[src, s], rp_s.at[src, s], rp_r.at[src, s], pts=src).wait_recv()
            mine = mine + rin[src, s].astype(F32)
        for i, t in enumerate(group[s]):
            red[t] = mine[:, i * tile:(i + 1) * tile]
            zsnd[t] = mine[:, i * tile:(i + 1) * tile].astype(BF16)
    rz = []
    for k in range(1, nm):
        to = lax.rem(m + k, nm)
        c = remote(zsnd.at[to], zin.at[k - 1], rz_s.at[k - 1], rz_r.at[k - 1], mat=to)
        c.start()
        rz.append(c)
    mine = red[m]
    for k in range(1, nm):
        rz[k - 1].wait_recv()
        mine = mine + zin[k - 1].astype(F32)
    out_pot[...] = mine.astype(BF16)

    for c in ag + fw + cs + cz + cg + rz:
        c.wait_send()
    for to in range(npts):
        for s in range(2):
            c = remote(snd.at[to, s], rin.at[p, s], rp_s.at[to, s], rp_r.at[p, s], pts=to)

            @pl.when(to != p)
            def _():
                c.wait_send()


def shards(
    nm, npts,
    basis_values, tile_ids, density_matrix, descriptors, grid_weights, centre_ids,
    density_scale, norm_gain, w_first, b_first, w_second, b_second, w_third, b_third,
):
    batches, points, orbitals = basis_values.shape
    per_batch = tile_ids.shape[1]
    tile = orbitals // per_batch
    rows, nb = density_matrix.shape
    feat = descriptors.shape[2]
    hid = w_first.shape[1]
    ntile = nb // tile
    cent = 16
    ncent = cent * npts
    slab = nb // npts
    width = nb // nm
    factor = ntile / (per_batch * math.sqrt(points * feat * batches * nm * npts))
    vm = pl.BlockSpec(memory_space=pltpu.VMEM)
    anyw = pl.BlockSpec(memory_space=pl.ANY)
    fp = feat // npts
    dma = pltpu.SemaphoreType.DMA
    nfw = (nm - 1) * (SPLIT - 1)
    potential, centre_features = pl.pallas_call(
        functools.partial(kernel, nm, npts, factor),
        out_shape=(
            jax.ShapeDtypeStruct((slab, width), BF16),
            jax.ShapeDtypeStruct((cent, feat), BF16),
        ),
        in_specs=[anyw] * 14,
        out_specs=(vm, vm),
        scratch_shapes=[
            pltpu.SMEM((batches, per_batch), jnp.int32),
            pltpu.VMEM((rows, nb), BF16),
            pltpu.VMEM((batches, points), F32),
            pltpu.VMEM((batches, points), jnp.int32),
            pltpu.VMEM((1, feat), F32),
            pltpu.VMEM((1, feat), F32),
            pltpu.VMEM((feat, hid), BF16),
            pltpu.VMEM((1, hid), F32),
            pltpu.VMEM((hid, hid), BF16),
            pltpu.VMEM((1, hid), F32),
            pltpu.VMEM((feat, hid), BF16),
            pltpu.VMEM((1, feat), F32),
            [pltpu.VMEM((per_batch, points, tile), BF16) for _ in range(batches)],
            pltpu.VMEM((batches, feat, points), BF16),
            pltpu.VMEM((batches, nb, points), BF16),
            pltpu.VMEM((batches, ncent, points), BF16),
            pltpu.VMEM((batches, 1, points), F32),
            pltpu.VMEM((batches, 1, points), F32),
            pltpu.VMEM((nb, nb), BF16),
            pltpu.VMEM((feat, ncent), F32),
            pltpu.VMEM((npts, fp, ncent), F32),
            pltpu.VMEM((npts, fp, ncent), F32),
            pltpu.VMEM((fp, ncent), F32),
            pltpu.VMEM((nm, fp, ncent), F32),
            pltpu.VMEM((npts, fp, ncent), F32),
            pltpu.VMEM((ncent, feat), F32),
            pltpu.VMEM((feat, ncent), BF16),
            pltpu.VMEM((npts, 2, slab, nb // 2), F32),
            pltpu.VMEM((npts, 2, slab, nb // 2), BF16),
            pltpu.VMEM((npts, 2, slab, nb // 2), BF16),
            pltpu.VMEM((nm, slab, width), F32),
            pltpu.VMEM((nm, slab, width), BF16),
            pltpu.VMEM((nm, slab, width), BF16),
            dma((12,)), dma((batches, per_batch)), dma((batches,)),
            dma((nm,)), dma((nm,)),
            dma((nfw,)), dma((nfw,)),
            dma((npts - 1,)), dma((npts - 1,)),
            dma((nm - 1,)), dma((nm - 1,)),
            dma((npts - 1,)), dma((npts - 1,)),
            dma((npts, 2)), dma((npts, 2)),
            dma((nm - 1,)), dma((nm - 1,)),
        ],
        compiler_params=pltpu.CompilerParams(
            collective_id=0, has_side_effects=True, vmem_limit_bytes=60 * 1024 * 1024
        ),
    )(
        basis_values, descriptors.transpose(0, 2, 1), tile_ids, density_matrix, grid_weights, centre_ids,
        density_scale.reshape(1, -1), norm_gain.reshape(1, -1),
        w_first, b_first.reshape(1, -1), w_second, b_second.reshape(1, -1),
        w_third.T, b_third.reshape(1, -1),
    )
    potential, centre_features = pl.pallas_call(
        place,
        out_shape=(
            jax.ShapeDtypeStruct((slab, width), BF16),
            jax.ShapeDtypeStruct((cent, feat), BF16),
        ),
        in_specs=[vm, vm],
        out_specs=(vm, vm),
    )(potential, centre_features)
    return (potential.T, centre_features)


def solution(mesh):
    return jax.shard_map(
        functools.partial(shards, mesh.shape["mat"], mesh.shape["pts"]),
        mesh=mesh,
        in_specs=(
            P(("mat", "pts"), None, None),
            P(("mat", "pts"), None),
            P("mat", None),
            P(("mat", "pts"), None, None),
            P(("mat", "pts"), None),
            P(("mat", "pts"), None),
            P(), P(), P(), P(), P(), P(), P(), P(),
        ),
        out_specs=(P("mat", "pts"), P("pts", None)),
        check_vma=False,
    )
```

time: 61 us -> 47.6 us (0.78)
  the two profiles are of different devices: /device:TPU:4 before, /device:TPU:0 now
where the time goes in v1:
time: 47.6 us; the launch traced here: 47.4 us
  Pallas kernels  46.7 us (98%)
  between operations  0.64 us (1%)
    pallas_call x1, Pallas kernels, shards(): pl.pallas_call(functools.partial(kernel, nm, npts, factor), out_shape=(ja...  45.4 us
    pallas_call x1, Pallas kernels, shards(): pl.pallas_call(place, out_shape=(jax.ShapeDtypeStruct((slab, width), BF16...  1.33 us

profile of v1, /device:TPU:0, one launch (start us, length us, event | category | flops | bytes accessed | tf_op | source)
XLA Modules:
  0.0 47.4 jit_solution(9166204987822002157)
XLA Ops:
  0.6 45.4 %shard_map.149 = (bf16[64,128]{1,0:T(8,128)(2,1)}, bf16[16,64]{1,0:T(8,128)(2,1)}) custom-call(bf16[4,2048,512]{2,1,0:T(8,128)(2,1)} %v_hbm.1, bf16[4,64,2048]{2,1,0:T(8,128)(2,1)} %bitcast.8, s32[4,4]{1,0:T(4,128)} %tiles_hbm.1, bf16[128,512]{1,0:T(8,128)(2,1)} %dm_hbm.1, f32[4,2048]{1,0:T(4,128)} %gw_hbm.1, s32[4,2048]{1,0:T(4,128)} %ids_hbm.1, ...), custom_call_target="tpu_custom_call" | custom-call | tf_op jit(solution)/shard_map/pallas_call | solution.py:343
  46.0 1.3 %shard_map.150 = (bf16[64,128]{1,0:T(8,128)(2,1)}, bf16[16,64]{1,0:T(8,128)(2,1)}) custom-call(bf16[64,128]{1,0:T(8,128)(2,1)} %get-tuple-element.6.pot, bf16[16,64]{1,0:T(8,128)(2,1)} %get-tuple-element.7.cf), custom_call_target="tpu_custom_call" | custom-call | tf_op jit(solution)/shard_map/pallas_call | solution.py:403

commit v2 on v1

--- a/solution.py
+++ b/solution.py
@@ -31,16 +31,16 @@
     v_hbm, d_hbm, tiles_hbm, dm_hbm, gw_hbm, ids_hbm, scale_hbm, gain_hbm,
     w1_hbm, b1_hbm, w2_hbm, b2_hbm, w3_hbm, b3_hbm,
     out_pot, out_cf,
-    tiles, dm, gw, ids, scale, gain, w1, b1, w2, b2, w3, b3,
+    tiles, gw, ids, scale, gain, w1, b1, w2, b2, w3, b3,
     vbuf, dbuf, vt, oh, dens, pps, panel, cpart, cs_src, cs_in, cz_src, cz_in,
-    full, cf_s, cft, acc, snd, rin, red, zsnd, zin,
-    isem, vsem, dsem, ag_s, ag_r, fw_s, fw_r, cs_s, cs_r, cz_s, cz_r, cg_s, cg_r, rp_s, rp_r, rz_s, rz_r,
+    full, cf_s, cft, acc, psnd, pin, whole, snd, rin, red, zsnd, zin,
+    isem, vsem, dsem, ag_s, ag_r, fw_s, fw_r, cs_s, cs_r, cz_s, cz_r, cg_s, cg_r, pr_s, pr_r, rp_s, rp_r, rz_s, rz_r,
 ):
     m = lax.axis_index("mat")
     p = lax.axis_index("pts")
     batches = len(vbuf)
     per_batch, points, tile = vbuf[0].shape
-    rows, nb = dm.shape
+    rows, nb = dm_hbm.shape
     ntile = nb // tile
     feat = dbuf.shape[1]
     ncent = oh.shape[1]
@@ -50,7 +50,8 @@
 
     small = [
         pltpu.make_async_copy(a, b, isem.at[i]) for i, (a, b) in enumerate((
-            (tiles_hbm, tiles), (dm_hbm, dm), (ids_hbm, ids), (gw_hbm, gw), (scale_hbm, scale), (gain_hbm, gain),
+            (tiles_hbm, tiles), (ids_hbm, ids), (dm_hbm, panel.at[pl.ds(pl.multiple_of(m * rows, rows), rows)]),
+            (gw_hbm, gw), (scale_hbm, scale), (gain_hbm, gain),
             (w1_hbm, w1), (b1_hbm, b1), (w2_hbm, w2), (b2_hbm, b2), (w3_hbm, w3), (b3_hbm, b3)))]
 
     def vcopy(b, j):
@@ -64,19 +65,9 @@
         pl.semaphore_signal(barrier, inc=1, device_id={"pts": lax.rem(p + k, npts)}, device_id_type=MESH)
     for k in range(1, nm):
         pl.semaphore_signal(barrier, inc=1, device_id={"mat": lax.rem(m + k, nm)}, device_id_type=MESH)
-    for c in small[:3]:
-        c.start()
+    small[0].start()
     for j in range(per_batch):
         vcopy(0, j).start()
-    for c in small[3:]:
-        c.start()
-    for b in range(1, batches):
-        for j in range(per_batch):
-            vcopy(b, j).start()
-    for b in range(batches):
-        dcopy(b).start()
-    for c in small[:3]:
-        c.wait()
     pl.semaphore_wait(barrier, npts + nm - 2)
 
     def remote(src, dst, s, r, **where):
@@ -89,17 +80,27 @@
 
     g = lax.rem(p, SPLIT)
     base = p - g
-    peer = [lax.rem(m + k, nm) for k in range(nm)]
     near = m + 1 - 2 * lax.rem(m, 2)
     order = [near] + [lax.rem(m + 2 * (k // 2) + lax.rem(m + k, 2) - lax.rem(m, 2) + nm, nm) for k in range(2, nm)]
     ag = []
     for k, to in enumerate(order):
         ag.append(remote(
-            dm.at[pl.ds(pl.multiple_of(g * piece, piece), piece)], panel.at[at_rows(m, g)],
+            dm_hbm.at[pl.ds(pl.multiple_of(g * piece, piece), piece)], panel.at[at_rows(m, g)],
             ag_s.at[to], ag_r.at[m], mat=to))
     for c in ag:
         c.start()
-    panel[pl.ds(pl.multiple_of(m * rows, rows), rows), :] = dm[...]
+    for c in small[1:3]:
+        c.start()
+    for b in range(1, batches):
+        for j in range(per_batch):
+            vcopy(b, j).start()
+    for c in small[3:]:
+        c.start()
+    for b in range(batches):
+        dcopy(b).start()
+    small[0].wait()
+    small[1].wait()
+    small[2].wait()
 
     def prepare(b):
         for j in range(per_batch):
@@ -139,7 +140,7 @@
 
     def receive(k):
         src = order[k]
-        remote(dm.at[pl.ds(0, piece)], panel.at[at_rows(src, g)], ag_s.at[src], ag_r.at[src], mat=src).wait_recv()
+        remote(dm_hbm.at[pl.ds(0, piece)], panel.at[at_rows(src, g)], ag_s.at[src], ag_r.at[src], mat=src).wait_recv()
         held = panel.at[at_rows(src, g)]
         mine = []
         for s in range(1, SPLIT):
@@ -150,30 +151,24 @@
         fw.extend(mine)
         return mine
 
-    def part(b, pair):
-        at = pl.ds(pl.multiple_of(pair * 2 * rows, 2 * rows), 2 * rows)
+    def part(b, owner):
+        at = pl.ds(pl.multiple_of(owner * rows, rows), rows)
         q = jnp.dot(panel[at, :], vt[b], preferred_element_type=F32)
         return jnp.sum(q * vt[b, at, :].astype(F32), axis=0, keepdims=True)
 
-    pairs = nm // 2
-    own = m // 2
-    for c in receive(0):
+    passing = receive(0)
+    for b in range(batches):
+        dens[b] = part(b, m)
+    for k in range(nm - 2):
+        for c in passing:
+            c.wait_recv()
+        passing = receive(k + 1)
+        for b in range(batches):
+            dens[b] += part(b, order[k])
+    for c in passing:
         c.wait_recv()
-
-    def first(b, carry):
-        dens[b] = part(b, own)
-        return carry
-
-    lax.fori_loop(0, batches, first, 0)
-    for k in range(1, nm - 1):
-        receive(k)
-    for c in fw[SPLIT - 1:]:
-        c.wait_recv()
-
-    def second(b, carry):
-        d = dens[b]
-        for k in range(1, pairs):
-            d = d + part(b, lax.rem(own + k, pairs))
+    for b in range(batches):
+        d = dens[b] + part(b, order[nm - 2])
         dens[b] = d
         dcopy(b).wait()
         wf = gw[pl.ds(b, 1), :] * silu(d * scale_col + dbuf[b].astype(F32))
@@ -182,27 +177,24 @@
         both = lax.dot_general(
             jnp.concatenate([high, low], axis=0), oh[b], NT_DIMS, preferred_element_type=F32)
         cpart[...] += both[:feat] + both[feat:]
-        return carry
-
-    lax.fori_loop(0, batches, second, 0)
-
+
+    around = [lax.rem(p + k, npts) for k in sorted(range(1, npts), key=lambda k: -min(k, npts - k))]
     fp = feat // npts
     for i in range(npts):
         cs_src[i] = cpart[i * fp:(i + 1) * fp, :]
     cs = []
-    for k in range(1, npts):
-        to = lax.rem(p + k, npts)
-        c = remote(cs_src.at[to], cs_in.at[k - 1], cs_s.at[k - 1], cs_r.at[k - 1], pts=to)
+    for to in around:
+        c = remote(cs_src.at[to], cs_in.at[p], cs_s.at[to], cs_r.at[p], pts=to)
         c.start()
         cs.append(c)
     mine = cs_src[p]
-    for k in range(1, npts):
-        cs[k - 1].wait_recv()
-        mine = mine + cs_in[k - 1]
+    for src in around[::-1]:
+        remote(cs_src.at[src], cs_in.at[src], cs_s.at[src], cs_r.at[src], pts=src).wait_recv()
+        mine = mine + cs_in[src]
     cz_src[...] = mine
     cz = []
-    for k in range(1, nm):
-        c = remote(cz_src, cz_in.at[m], cz_s.at[k - 1], cz_r.at[k - 1], mat=lax.rem(m + k, nm))
+    for k, to in enumerate(order[::-1]):
+        c = remote(cz_src, cz_in.at[m], cz_s.at[k], cz_r.at[k], mat=to)
         c.start()
         cz.append(c)
     cz_in[m] = mine
@@ -213,12 +205,12 @@
         total = total + cz_in[i]
     full[p] = total
     cg = []
-    for k in range(1, npts):
-        c = remote(full.at[p], full.at[p], cg_s.at[k - 1], cg_r.at[k - 1], pts=lax.rem(p + k, npts))
+    for to in around:
+        c = remote(full.at[p], full.at[p], cg_s.at[to], cg_r.at[p], pts=to)
         c.start()
         cg.append(c)
-    for c in cg:
-        c.wait_recv()
+    for src in around[::-1]:
+        remote(full.at[src], full.at[src], cg_s.at[src], cg_r.at[src], pts=src).wait_recv()
 
     summed = jnp.concatenate([full[i] for i in range(npts)], axis=0).T
     inverse = lax.rsqrt(jnp.mean(summed * summed, axis=1, keepdims=True) + 1e-05)
@@ -231,91 +223,127 @@
     cent = out_cf.shape[0]
     out_cf[...] = cf_s[pl.ds(pl.multiple_of(p * cent, cent), cent), :].astype(BF16)
 
-    group = [[t for t in range(ntile) if (t + t // 2) % 2 == s] for s in range(2)]
-    per_tile = tile // slab
-    owners = [[t * per_tile + i for t in group[s] for i in range(per_tile)] for s in range(2)]
-    width = nb // nm
-    half = nb // 2
-    acc[...] = jnp.zeros_like(acc)
-
-    def side(b, s):
-        return jnp.concatenate([vt[b, t * tile:(t + 1) * tile, :] for t in group[s]], axis=0)
-
-    def block0(b, carry):
+    def spot(u, i):
+        return 2 * i + (i + u) % 2 if isinstance(u, int) else 2 * i + lax.rem(i + u, 2)
+
+    pairs = npts // 2
+    mid = pairs // 2
+    core = lax.rem(p, 2)
+    chip = p // 2
+    buddy = p + 1 - 2 * core
+
+    for b in range(batches):
         nearest = jnp.dot(cft[...], oh[b], preferred_element_type=F32)
         along = jnp.sum(nearest * dbuf[b].astype(F32), axis=0, keepdims=True)
-        pp = gw[pl.ds(b, 1), :] * dens[b] * along * factor
-        pps[b] = pp
-        w = (side(b, 0).astype(F32) * pp).astype(BF16)
-        r = lax.dot_general(w, side(b, 0), NT_DIMS, preferred_element_type=F32)
-        for i, o in enumerate(owners[0]):
-            acc[o, 0] += r[i * slab:(i + 1) * slab]
-        r = lax.dot_general(w, side(b, 1), NT_DIMS, preferred_element_type=F32)
-        for i, o in enumerate(owners[0]):
-            acc[o, 1] += r[i * slab:(i + 1) * slab]
+        pps[b] = gw[pl.ds(b, 1), :] * dens[b] * along * factor
+
+    def side(b, u):
+        return jnp.concatenate([
+            vt[b, pl.ds(pl.multiple_of(spot(u, i) * tile, tile), tile), :] for i in range(mid)], axis=0)
+
+    def quarter(u, w):
+        r = 0
+        for b in range(batches):
+            left = (side(b, u).astype(F32) * pps[b]).astype(BF16)
+            r = r + lax.dot_general(left, side(b, w), NT_DIMS, preferred_element_type=F32)
+        return r
+
+    def keep(r, first):
+        for i in range(mid):
+            for q in range(2):
+                acc[q, first + i] = r[(2 * i + q) * slab:(2 * i + q + 1) * slab]
+
+    stages = [
+        (0, [(spot(0, i), 1) for i in range(mid)] + [(spot(1, i), 0) for i in range(mid)]),
+        (2 * mid, [(spot(0, i), 0) for i in range(mid)]),
+        (3 * mid, [(spot(1, i), 1) for i in range(mid)]),
+    ]
+
+    def pair(n):
+        first, entries = stages[n]
+        at = pl.ds(first, len(entries))
+        return remote(psnd.at[at], pin.at[at], pr_s.at[n], pr_r.at[n], pts=buddy)
+
+    def give(n):
+        first, entries = stages[n]
+        for e in range(first, first + len(entries)):
+            psnd[e] = acc[1 - core, e].astype(BF16)
+        pair(n).start()
+
+    def plane(to, u):
+        return remote(snd.at[to, u], rin.at[chip, u], rp_s.at[to, u], rp_r.at[chip, u], pts=2 * to + core)
+
+    def spread(n):
+        first, entries = stages[n]
+        pair(n).wait_recv()
+        for e, (to, u) in enumerate(entries):
+            both = acc[core, first + e] + pin[first + e].astype(F32)
+            whole[to, u] = both
+            snd[to, u] = both.astype(BF16)
+        for to, u in entries:
+            @pl.when(to != chip)
+            def _():
+                plane(to, u).start()
+
+
+    def turn(n, carry):
+        keep(quarter(n // 2, jnp.where(n == 1, 0, 1)), jnp.where(n == 0, 0, (n + 1) * mid))
+
+        @pl.when(n == 0)
+        def _():
+            across = jnp.concatenate([acc[q, i] for i in range(mid) for q in range(2)], axis=0)
+            keep(across.T, mid)
+            give(0)
+
+        @pl.when(n == 1)
+        def _():
+            spread(0)
+            give(1)
+
+        @pl.when(n == 2)
+        def _():
+            give(2)
+            spread(1)
+
         return carry
 
-    def block1(b, carry):
-        x = side(b, 1)
-        w = (x.astype(F32) * pps[b]).astype(BF16)
-        r = lax.dot_general(w, x, NT_DIMS, preferred_element_type=F32)
-        for i, o in enumerate(owners[1]):
-            acc[o, 1] += r[i * slab:(i + 1) * slab]
-        return carry
-
-    def send(to, s):
-        c = remote(snd.at[to, s], rin.at[p, s], rp_s.at[to, s], rp_r.at[p, s], pts=to)
-
-        @pl.when(to != p)
-        def _():
-            c.start()
-
-    lax.fori_loop(0, batches, block0, 0)
-    for o in owners[0]:
-        snd[o, 0] = acc[o, 0].astype(BF16)
-        snd[o, 1] = acc[o, 1].astype(BF16)
-    across = jnp.concatenate([acc[o, 1] for o in owners[0]], axis=0).T
-    for i, o in enumerate(owners[1]):
-        acc[o, 0] = across[i * slab:(i + 1) * slab]
-        snd[o, 0] = across[i * slab:(i + 1) * slab].astype(BF16)
-    for o in range(npts):
-        send(o, 0)
-        if o in owners[0]:
-            send(o, 1)
-    lax.fori_loop(0, batches, block1, 0)
-    for o in owners[1]:
-        snd[o, 1] = acc[o, 1].astype(BF16)
-        send(o, 1)
-    for s in range(2):
-        mine = acc[p, s]
-        for k in range(1, npts):
-            src = lax.rem(p + k, npts)
-            remote(snd.at[src, s], rin.at[src, s], rp_s.at[src, s], rp_r.at[src, s], pts=src).wait_recv()
-            mine = mine + rin[src, s].astype(F32)
-        for i, t in enumerate(group[s]):
-            red[t] = mine[:, i * tile:(i + 1) * tile]
-            zsnd[t] = mine[:, i * tile:(i + 1) * tile].astype(BF16)
-    rz = []
+    lax.fori_loop(0, 3, turn, 0)
+    spread(2)
+    early = lax.rem(chip + chip // 2 + 1, 2)
+    for n in range(2):
+        u = early if n == 0 else 1 - early
+        mine = whole[chip, u]
+        for k in range(1, pairs):
+            src = lax.rem(chip + k, pairs)
+            remote(snd.at[src, u], rin.at[src, u], rp_s.at[src, u], rp_r.at[src, u], pts=2 * src + core).wait_recv()
+            mine = mine + rin[src, u].astype(F32)
+        for i in range(mid):
+            to = 2 * i + lax.rem(i + u, 2)
+            red[to] = mine[:, i * tile:(i + 1) * tile]
+            zsnd[to] = mine[:, i * tile:(i + 1) * tile].astype(BF16)
+
+            @pl.when(to != m)
+            def _():
+                remote(zsnd.at[to], zin.at[m], rz_s.at[to], rz_r.at[m], mat=to).start()
+    mine = red[m]
+    for k in range(1, nm):
+        src = lax.rem(m + k, nm)
+        remote(zsnd.at[src], zin.at[src], rz_s.at[src], rz_r.at[src], mat=src).wait_recv()
+        mine = mine + zin[src].astype(F32)
+    out_pot[...] = mine.astype(BF16)
+
+    for c in ag + fw + cs + cz + cg:
+        c.wait_send()
+    for n in range(len(stages)):
+        pair(n).wait_send()
+    for to in range(pairs):
+        for u in range(2):
+            @pl.when(to != chip)
+            def _():
+                plane(to, u).wait_send()
     for k in range(1, nm):
         to = lax.rem(m + k, nm)
-        c = remote(zsnd.at[to], zin.at[k - 1], rz_s.at[k - 1], rz_r.at[k - 1], mat=to)
-        c.start()
-        rz.append(c)
-    mine = red[m]
-    for k in range(1, nm):
-        rz[k - 1].wait_recv()
-        mine = mine + zin[k - 1].astype(F32)
-    out_pot[...] = mine.astype(BF16)
-
-    for c in ag + fw + cs + cz + cg + rz:
-        c.wait_send()
-    for to in range(npts):
-        for s in range(2):
-            c = remote(snd.at[to, s], rin.at[p, s], rp_s.at[to, s], rp_r.at[p, s], pts=to)
-
-            @pl.when(to != p)
-            def _():
-                c.wait_send()
+        remote(zsnd.at[to], zin.at[m], rz_s.at[to], rz_r.at[m], mat=to).wait_send()
 
 
 def shards(
@@ -350,7 +378,6 @@
         out_specs=(vm, vm),
         scratch_shapes=[
             pltpu.SMEM((batches, per_batch), jnp.int32),
-            pltpu.VMEM((rows, nb), BF16),
             pltpu.VMEM((batches, points), F32),
             pltpu.VMEM((batches, points), jnp.int32),
             pltpu.VMEM((1, feat), F32),
@@ -376,20 +403,24 @@
             pltpu.VMEM((npts, fp, ncent), F32),
             pltpu.VMEM((ncent, feat), F32),
             pltpu.VMEM((feat, ncent), BF16),
-            pltpu.VMEM((npts, 2, slab, nb // 2), F32),
-            pltpu.VMEM((npts, 2, slab, nb // 2), BF16),
-            pltpu.VMEM((npts, 2, slab, nb // 2), BF16),
+            pltpu.VMEM((2, npts, slab, nb // 2), F32),
+            pltpu.VMEM((npts, slab, nb // 2), BF16),
+            pltpu.VMEM((npts, slab, nb // 2), BF16),
+            pltpu.VMEM((npts // 2, 2, slab, nb // 2), F32),
+            pltpu.VMEM((npts // 2, 2, slab, nb // 2), BF16),
+            pltpu.VMEM((npts // 2, 2, slab, nb // 2), BF16),
             pltpu.VMEM((nm, slab, width), F32),
             pltpu.VMEM((nm, slab, width), BF16),
             pltpu.VMEM((nm, slab, width), BF16),
             dma((12,)), dma((batches, per_batch)), dma((batches,)),
             dma((nm,)), dma((nm,)),
             dma((nfw,)), dma((nfw,)),
-            dma((npts - 1,)), dma((npts - 1,)),
+            dma((npts,)), dma((npts,)),
             dma((nm - 1,)), dma((nm - 1,)),
-            dma((npts - 1,)), dma((npts - 1,)),
-            dma((npts, 2)), dma((npts, 2)),
-            dma((nm - 1,)), dma((nm - 1,)),
+            dma((npts,)), dma((npts,)),
+            dma((3,)), dma((3,)),
+            dma((npts // 2, 2)), dma((npts // 2, 2)),
+            dma((nm,)), dma((nm,)),
         ],
         compiler_params=pltpu.CompilerParams(
             collective_id=0, has_side_effects=True, vmem_limit_bytes=60 * 1024 * 1024

time: 47.6 us -> 43.8 us (0.920)
  Pallas kernels: 46.7 us -> 42.9 us
    pallas_call x1, Pallas kernels: 45.4 us -> 41.6 us  [shards(): pl.pallas_call(functools.partial(kernel, nm, npts, factor), out_shape=(ja...]
where the time goes in v2:
time: 43.8 us; the launch traced here: 43.5 us
  Pallas kernels  42.9 us (98%)
  between operations  0.64 us (1%)
    pallas_call x1, Pallas kernels, shards(): pl.pallas_call(functools.partial(kernel, nm, npts, factor), out_shape=(ja...  41.6 us
    pallas_call x1, Pallas kernels, shards(): pl.pallas_call(place, out_shape=(jax.ShapeDtypeStruct((slab, width), BF16...  1.33 us

profile of v2, /device:TPU:0, one launch (start us, length us, event | category | flops | bytes accessed | tf_op | source)
XLA Modules:
  0.0 43.5 jit_solution(5173264340549019732)
XLA Ops:
  0.6 41.6 %shard_map.149 = (bf16[64,128]{1,0:T(8,128)(2,1)}, bf16[16,64]{1,0:T(8,128)(2,1)}) custom-call(bf16[4,2048,512]{2,1,0:T(8,128)(2,1)} %v_hbm.1, bf16[4,64,2048]{2,1,0:T(8,128)(2,1)} %bitcast.8, s32[4,4]{1,0:T(4,128)} %tiles_hbm.1, bf16[128,512]{1,0:T(8,128)(2,1)} %dm_hbm.1, f32[4,2048]{1,0:T(4,128)} %gw_hbm.1, s32[4,2048]{1,0:T(4,128)} %ids_hbm.1, ...), custom_call_target="tpu_custom_call" | custom-call | tf_op jit(solution)/shard_map/pallas_call | solution.py:371
  42.2 1.3 %shard_map.150 = (bf16[64,128]{1,0:T(8,128)(2,1)}, bf16[16,64]{1,0:T(8,128)(2,1)}) custom-call(bf16[64,128]{1,0:T(8,128)(2,1)} %get-tuple-element.6.pot, bf16[16,64]{1,0:T(8,128)(2,1)} %get-tuple-element.7.cf), custom_call_target="tpu_custom_call" | custom-call | tf_op jit(solution)/shard_map/pallas_call | solution.py:434

commit v3 on v2

v3 whole, which is shorter than its diff:
```python
import functools
import math

import jax
import jax.numpy as jnp
from jax import lax
from jax.experimental import pallas as pl
from jax.experimental.pallas import tpu as pltpu
from jax.sharding import PartitionSpec as P

SPLIT = 2
MESH = pl.DeviceIdType.MESH
F32 = jnp.float32
BF16 = jnp.bfloat16
NT_DIMS = (((1,), (1,)), ((), ()))


def silu(v):
    h = 0.5 * v
    return h + h * jnp.tanh(h)


def place(pot, cf, out_pot, out_cf, sem):
    copies = [pltpu.make_async_copy(pot, out_pot, sem.at[0]), pltpu.make_async_copy(cf, out_cf, sem.at[1])]
    for c in copies:
        c.start()
    for c in copies:
        c.wait()


def kernel(
    nm, npts, factor,
    v_hbm, d_hbm, tiles_hbm, dm_hbm, gw_hbm, ids_hbm, scale_hbm, gain_hbm,
    w1_hbm, b1_hbm, w2_hbm, b2_hbm, w3_hbm, b3_hbm,
    out_pot, out_cf,
    tiles, gw, ids, w13, b12, sgb, w2,
    vbuf, dbuf, vt, oh, dens, pps, panel, cpart, cs_src, cs_in, cz_src, cz_in,
    full, cf_s, cft, acc, psnd, pin, whole, snd, rin, red, zsnd, zin,
    isem, msem, vsem, ag_s, ag_r, fw_s, fw_r, cs_s, cs_r, cz_s, cz_r, cg_s, cg_r, pr_s, pr_r, rp_s, rp_r, rz_s, rz_r,
):
    m = lax.axis_index("mat")
    p = lax.axis_index("pts")
    batches = len(vbuf)
    per_batch, points, tile = vbuf[0].shape
    rows, nb = dm_hbm.shape
    ntile = nb // tile
    feat = dbuf.shape[1]
    ncent = oh.shape[1]
    slab = nb // npts
    piece = rows // SPLIT

    small = [
        pltpu.make_async_copy(a, b, isem.at[i]) for i, (a, b) in enumerate((
            (tiles_hbm, tiles), (ids_hbm, ids), (dm_hbm, panel.at[pl.ds(pl.multiple_of(m * rows, rows), rows)]),
            (gw_hbm, gw), (w2_hbm, w2), (d_hbm, dbuf)))]
    grouped = [
        pltpu.make_async_copy(a, b, msem.at[i]) for a, b, i in (
            (w1_hbm, w13.at[0], 0), (w3_hbm, w13.at[1], 0), (b1_hbm, b12.at[0], 1), (b2_hbm, b12.at[1], 1),
            (scale_hbm, sgb.at[0], 2), (gain_hbm, sgb.at[1], 2), (b3_hbm, sgb.at[2], 2))]

    def vcopy(b, j):
        return pltpu.make_async_copy(v_hbm.at[b, :, pl.ds(j * tile, tile)], vbuf[b].at[j], vsem.at[b])

    barrier = pltpu.get_barrier_semaphore()
    for k in range(1, npts):
        pl.semaphore_signal(barrier, inc=1, device_id={"pts": lax.rem(p + k, npts)}, device_id_type=MESH)
    for k in range(1, nm):
        pl.semaphore_signal(barrier, inc=1, device_id={"mat": lax.rem(m + k, nm)}, device_id_type=MESH)
    for c in small[:3]:
        c.start()
    for j in range(per_batch):
        vcopy(0, j).start()
    pl.semaphore_wait(barrier, npts + nm - 2)

    def remote(src, dst, s, r, **where):
        return pltpu.make_async_remote_copy(
            src_ref=src, dst_ref=dst, send_sem=s, recv_sem=r, device_id=where, device_id_type=MESH
        )

    def at_rows(owner, part):
        return pl.ds(pl.multiple_of(owner * rows + part * piece, piece), piece)

    g = lax.rem(p, SPLIT)
    base = p - g
    near = m + 1 - 2 * lax.rem(m, 2)
    order = [near] + [lax.rem(m + 2 * (k // 2) + lax.rem(m + k, 2) - lax.rem(m, 2) + nm, nm) for k in range(2, nm)]
    ag = []
    for k, to in enumerate(order):
        ag.append(remote(
            dm_hbm.at[pl.ds(pl.multiple_of(g * piece, piece), piece)], panel.at[at_rows(m, g)],
            ag_s, ag_r.at[m], mat=to))
    for c in ag:
        c.start()
    for b in range(1, batches):
        for j in range(per_batch):
            vcopy(b, j).start()
    for c in small[3:] + grouped:
        c.start()
    small[0].wait()

    def part(b, owner, which=slice(None)):
        at = pl.ds(pl.multiple_of(owner * rows, rows), rows)
        q = jnp.dot(panel[at, :], vt[b][:, which], preferred_element_type=F32)
        return jnp.sum(q * vt[b][at, which].astype(F32), axis=0, keepdims=True)

    def prepare(b):
        pltpu.make_async_copy(vbuf[b], vbuf[b], vsem.at[b]).wait()
        held = [tiles[b, j] for j in range(per_batch)]

        def find(t, value, otherwise):
            for j in range(per_batch):
                otherwise = jnp.where(held[j] == t, value(j), otherwise)
            return otherwise

        spot = [find(t, lambda j: j, 0) for t in range(ntile)]
        here = [find(t, lambda j: 1, 0) for t in range(ntile)]
        for t in range(ntile):
            x = vbuf[b][spot[t]]
            if ntile != per_batch:
                x = jnp.where(here[t] == 1, x, jnp.zeros_like(x))
            vt[b][t * tile:(t + 1) * tile, :] = x.T

    def mask(b):
        which = lax.broadcasted_iota(jnp.int32, (ncent, points), 0)
        oh[b] = jnp.where(which == ids[b:b + 1, :], 1.0, 0.0).astype(BF16)

    fw = []

    def ahead(k):
        src = order[k]
        return remote(
            dm_hbm.at[pl.ds(0, piece)], panel.at[at_rows(src, g)], ag_s, ag_r.at[src], mat=src)

    def receive(k):
        ahead(k).wait_recv()
        held = panel.at[at_rows(order[k], g)]
        mine = []
        for h in range(1, SPLIT):
            i = k * (SPLIT - 1) + h - 1
            c = remote(held, held, fw_s, fw_r.at[i], pts=base + lax.rem(g + h, SPLIT))
            c.start()
            mine.append(c)
        fw.extend(mine)
        return mine

    for b in range(batches):
        if b == 1:
            small[1].wait()
            small[2].wait()
        if b:
            dens[b - 1] = part(b - 1, m)
            mask(b - 1)
        prepare(b)
        if b == batches - 2:
            passing = receive(0)
    for c in small[3:]:
        c.wait()
    pltpu.make_async_copy(w13, w13, msem.at[0]).wait()
    pltpu.make_async_copy(b12, b12, msem.at[1]).wait()
    pltpu.make_async_copy(sgb, sgb, msem.at[2]).wait()
    scale, gain, b3 = sgb.at[0], sgb.at[1], sgb.at[2]
    w1, w3 = w13.at[0], w13.at[1]
    b1, b2 = b12.at[0], b12.at[1]

    scale_col = jnp.broadcast_to(scale[...], (128, feat)).T[:, :1]
    cpart[...] = jnp.zeros_like(cpart)

    dens[batches - 1] = part(batches - 1, m)
    mask(batches - 1)
    for k in range(nm - 2):
        for c in passing:
            c.wait_recv()
        passing = receive(k + 1)
        for b in range(batches):
            dens[b] += part(b, order[k])
    for c in passing:
        c.wait_recv()
    for b in range(batches):
        d = dens[b] + part(b, order[nm - 2])
        dens[b] = d
        wf = gw[pl.ds(b, 1), :] * silu(d * scale_col + dbuf[b].astype(F32))
        high = wf.astype(BF16)
        low = (wf - high.astype(F32)).astype(BF16)
        both = lax.dot_general(
            jnp.concatenate([high, low], axis=0), oh[b], NT_DIMS, preferred_element_type=F32)
        cpart[...] += both[:feat] + both[feat:]

    far = sorted(range(1, npts), key=lambda k: -min(k, npts - k))
    fp = feat // npts
    for i in range(npts):
        cs_src[i] = cpart[i * fp:(i + 1) * fp, :]
    for k in far:
        to = lax.rem(p + k, npts)
        remote(cs_src.at[to], cs_in.at[k - 1], cs_s, cs_r, pts=to).start()
    all_cs = remote(cs_in, cs_in, cs_s, cs_r, pts=lax.rem(p + 1, npts))
    all_cs.wait_recv()
    mine = cs_src[p]
    for k in range(1, npts):
        mine = mine + cs_in[k - 1]
    cz_src[...] = mine
    for k in sorted(range(1, nm), key=lambda k: -min(k, nm - k)):
        to = lax.rem(m + k, nm)
        remote(cz_src, cz_in.at[k - 1], cz_s, cz_r, mat=to).start()
    all_cz = remote(cz_in, cz_in, cz_s, cz_r, mat=lax.rem(m + 1, nm))
    all_cz.wait_recv()
    total = mine
    for k in range(1, nm):
        total = total + cz_in[k - 1]
    full[npts - 1] = total
    for k in far:
        remote(full.at[npts - 1], full.at[k - 1], cg_s, cg_r, pts=lax.rem(p + k, npts)).start()
    others = full.at[pl.ds(0, npts - 1)]
    all_cg = remote(others, others, cg_s, cg_r, pts=lax.rem(p + 1, npts))
    all_cg.wait_recv()

    summed = jnp.concatenate([full[lax.rem(p - i - 1 + npts, npts)] for i in range(npts)], axis=0).T
    inverse = lax.rsqrt(jnp.mean(summed * summed, axis=1, keepdims=True) + 1e-05)
    normed = (summed * inverse * gain[...]).astype(BF16)
    one = silu(jnp.dot(normed, w1[...], preferred_element_type=F32) + b1[...]).astype(BF16)
    two = silu(jnp.dot(one, w2[...], preferred_element_type=F32) + b2[...]).astype(BF16)
    cf = (lax.dot_general(two, w3[...], NT_DIMS, preferred_element_type=F32) + b3[...]).astype(BF16).astype(F32)
    cf_s[...] = cf
    cft[...] = cf.T.astype(BF16)
    cent = out_cf.shape[0]
    out_cf[...] = cf_s[pl.ds(pl.multiple_of(p * cent, cent), cent), :].astype(BF16)

    def spot(u, i):
        return 2 * i + (i + u) % 2 if isinstance(u, int) else 2 * i + lax.rem(i + u, 2)

    pairs = npts // 2
    mid = pairs // 2
    core = lax.rem(p, 2)
    chip = p // 2
    buddy = p + 1 - 2 * core

    for b in range(batches):
        nearest = jnp.dot(cft[...], oh[b], preferred_element_type=F32)
        along = jnp.sum(nearest * dbuf[b].astype(F32), axis=0, keepdims=True)
        pps[b] = gw[pl.ds(b, 1), :] * dens[b] * along * factor

    def side(b, u):
        return jnp.concatenate([
            vt[b][pl.ds(pl.multiple_of(spot(u, i) * tile, tile), tile), :] for i in range(mid)], axis=0)

    def quarter(u, w):
        r = 0
        for b in range(batches):
            left = (side(b, u).astype(F32) * pps[b]).astype(BF16)
            r = r + lax.dot_general(left, side(b, w), NT_DIMS, preferred_element_type=F32)
        return r

    def keep(r, first):
        for i in range(mid):
            for q in range(2):
                acc[q, first + i] = r[(2 * i + q) * slab:(2 * i + q + 1) * slab]

    stages = [
        (0, [(spot(0, i), 1) for i in range(mid)] + [(spot(1, i), 0) for i in range(mid)]),
        (2 * mid, [(spot(0, i), 0) for i in range(mid)]),
        (3 * mid, [(spot(1, i), 1) for i in range(mid)]),
    ]

    def pair(n):
        first, entries = stages[n]
        at = pl.ds(first, len(entries))
        return remote(psnd.at[at], pin.at[at], pr_s, pr_r.at[n], pts=buddy)

    def give(n):
        first, entries = stages[n]
        for e in range(first, first + len(entries)):
            psnd[e] = acc[1 - core, e].astype(BF16)
        pair(n).start()

    def plane(to, u):
        return remote(snd.at[to, u], rin.at[u, lax.rem(to - chip - 1 + pairs, pairs)], rp_s, rp_r.at[u], pts=2 * to + core)

    def spread(n):
        first, entries = stages[n]
        pair(n).wait_recv()
        for e, (to, u) in enumerate(entries):
            both = acc[core, first + e] + pin[first + e].astype(F32)
            whole[to, u] = both
            snd[to, u] = both.astype(BF16)
        for to, u in entries:
            @pl.when(to != chip)
            def _():
                plane(to, u).start()


    def turn(n, carry):
        keep(quarter(n // 2, jnp.where(n == 1, 0, 1)), jnp.where(n == 0, 0, (n + 1) * mid))

        @pl.when(n == 0)
        def _():
            across = jnp.concatenate([acc[q, i] for i in range(mid) for q in range(2)], axis=0)
            keep(across.T, mid)
            give(0)

        @pl.when(n == 1)
        def _():
            spread(0)
            give(1)

        @pl.when(n == 2)
        def _():
            give(2)
            spread(1)

        return carry

    lax.fori_loop(0, 3, turn, 0)
    spread(2)
    early = lax.rem(chip + chip // 2 + 1, 2)
    for n in range(2):
        u = early if n == 0 else 1 - early
        mine = whole[chip, u]
        remote(rin.at[u], rin.at[u], rp_s, rp_r.at[u], pts=buddy).wait_recv()
        for k in range(pairs - 1):
            mine = mine + rin[u, k].astype(F32)
        for i in range(mid):
            to = 2 * i + lax.rem(i + u, 2)
            red[to] = mine[:, i * tile:(i + 1) * tile]
            zsnd[to] = mine[:, i * tile:(i + 1) * tile].astype(BF16)

            @pl.when(to != m)
            def _():
                remote(zsnd.at[to], zin.at[lax.rem(to - m - 1 + nm, nm)], rz_s, rz_r, mat=to).start()
    mine = red[m]
    all_rz = remote(zin, zin, rz_s, rz_r, mat=lax.rem(m + 1, nm))
    all_rz.wait_recv()
    for k in range(nm - 1):
        mine = mine + zin[k].astype(F32)
    out_pot[...] = mine.astype(BF16)

    for c in (all_cs, all_cz, all_cg, all_rz):
        c.wait_send()
    sent = panel.at[pl.ds(0, (nm - 1) * piece)]
    remote(sent, sent, ag_s, ag_r.at[m], mat=lax.rem(m + 1, nm)).wait_send()
    sent = panel.at[pl.ds(0, (nm - 1) * (SPLIT - 1) * piece)]
    remote(sent, sent, fw_s, fw_r.at[0], pts=buddy).wait_send()
    remote(psnd, pin, pr_s, pr_r.at[0], pts=buddy).wait_send()
    remote(rin, rin, rp_s, rp_r.at[0], pts=buddy).wait_send()


def shards(
    nm, npts,
    basis_values, tile_ids, density_matrix, descriptors, grid_weights, centre_ids,
    density_scale, norm_gain, w_first, b_first, w_second, b_second, w_third, b_third,
):
    batches, points, orbitals = basis_values.shape
    per_batch = tile_ids.shape[1]
    tile = orbitals // per_batch
    rows, nb = density_matrix.shape
    feat = descriptors.shape[2]
    hid = w_first.shape[1]
    ntile = nb // tile
    cent = 16
    ncent = cent * npts
    slab = nb // npts
    width = nb // nm
    factor = ntile / (per_batch * math.sqrt(points * feat * batches * nm * npts))
    vm = pl.BlockSpec(memory_space=pltpu.VMEM)
    anyw = pl.BlockSpec(memory_space=pl.ANY)
    fp = feat // npts
    dma = pltpu.SemaphoreType.DMA
    nfw = (nm - 1) * (SPLIT - 1)
    potential, centre_features = pl.pallas_call(
        functools.partial(kernel, nm, npts, factor),
        out_shape=(pltpu.VMEM((slab, width), BF16), pltpu.VMEM((cent, feat), BF16)),
        in_specs=[anyw] * 14,
        out_specs=(vm, vm),
        scratch_shapes=[
            pltpu.SMEM((batches, per_batch), jnp.int32),
            pltpu.VMEM((batches, points), F32),
            pltpu.VMEM((batches, points), jnp.int32),
            pltpu.VMEM((2, feat, hid), BF16),
            pltpu.VMEM((2, 1, hid), F32),
            pltpu.VMEM((3, 1, feat), F32),
            pltpu.VMEM((hid, hid), BF16),
            [pltpu.VMEM((per_batch, points, tile), BF16) for _ in range(batches)],
            pltpu.VMEM((batches, feat, points), BF16),
            [pltpu.VMEM((nb, points), BF16) for _ in range(batches)],
            pltpu.VMEM((batches, ncent, points), BF16),
            pltpu.VMEM((batches, 1, points), F32),
            pltpu.VMEM((batches, 1, points), F32),
            pltpu.VMEM((nb, nb), BF16),
            pltpu.VMEM((feat, ncent), F32),
            pltpu.VMEM((npts, fp, ncent), F32),
            pltpu.VMEM((npts - 1, fp, ncent), F32),
            pltpu.VMEM((fp, ncent), F32),
            pltpu.VMEM((nm - 1, fp, ncent), F32),
            pltpu.VMEM((npts, fp, ncent), F32),
            pltpu.VMEM((ncent, feat), F32),
            pltpu.VMEM((feat, ncent), BF16),
            pltpu.VMEM((2, npts, slab, nb // 2), F32),
            pltpu.VMEM((npts, slab, nb // 2), BF16),
            pltpu.VMEM((npts, slab, nb // 2), BF16),
            pltpu.VMEM((npts // 2, 2, slab, nb // 2), F32),
            pltpu.VMEM((npts // 2, 2, slab, nb // 2), BF16),
            pltpu.VMEM((2, npts // 2 - 1, slab, nb // 2), BF16),
            pltpu.VMEM((nm, slab, width), F32),
            pltpu.VMEM((nm, slab, width), BF16),
            pltpu.VMEM((nm - 1, slab, width), BF16),
            dma((6,)), dma((3,)), dma((batches,)),
            dma, dma((nm,)), dma, dma((nfw,)),
            dma, dma, dma, dma, dma, dma,
            dma, dma((3,)), dma, dma((2,)), dma, dma,
        ],
        compiler_params=pltpu.CompilerParams(
            collective_id=0, has_side_effects=True, vmem_limit_bytes=60 * 1024 * 1024
        ),
    )(
        basis_values, descriptors.transpose(0, 2, 1), tile_ids, density_matrix, grid_weights, centre_ids,
        density_scale.reshape(1, -1), norm_gain.reshape(1, -1),
        w_first, b_first.reshape(1, -1), w_second, b_second.reshape(1, -1),
        w_third.T, b_third.reshape(1, -1),
    )
    potential, centre_features = pl.pallas_call(
        place,
        out_shape=(
            jax.ShapeDtypeStruct((slab, width), BF16),
            jax.ShapeDtypeStruct((cent, feat), BF16),
        ),
        in_specs=[vm, vm],
        out_specs=(anyw, anyw),
        scratch_shapes=[dma((2,))],
    )(
        pltpu.with_memory_space_constraint(potential, pltpu.VMEM),
        pltpu.with_memory_space_constraint(centre_features, pltpu.VMEM),
    )
    return (potential.T, centre_features)


def solution(mesh):
    return jax.shard_map(
        functools.partial(shards, mesh.shape["mat"], mesh.shape["pts"]),
        mesh=mesh,
        in_specs=(
            P(("mat", "pts"), None, None),
            P(("mat", "pts"), None),
            P("mat", None),
            P(("mat", "pts"), None, None),
            P(("mat", "pts"), None),
            P(("mat", "pts"), None),
            P(), P(), P(), P(), P(), P(), P(), P(),
        ),
        out_specs=(P("mat", "pts"), P("pts", None)),
        check_vma=False,
    )
```

time: 43.8 us -> 41.3 us (0.943)
  Pallas kernels: 42.9 us -> 40.5 us
    pallas_call x1, Pallas kernels: 41.6 us -> 39.9 us  [shards(): pl.pallas_call(functools.partial(kernel, nm, npts, factor), out_shape=(pl...]
    pallas_call x1, Pallas kernels: 1.33 us -> 0.63 us  [shards(): pl.pallas_call(place, out_shape=(jax.ShapeDtypeStruct((slab, width), BF16...]
where the time goes in v3:
time: 41.3 us; the launch traced here: 41.2 us
  Pallas kernels  40.5 us (98%)
  between operations  0.64 us (2%)
    pallas_call x1, Pallas kernels, shards(): pl.pallas_call(functools.partial(kernel, nm, npts, factor), out_shape=(pl...  39.9 us

profile of v3, /device:TPU:0, one launch (start us, length us, event | category | flops | bytes accessed | tf_op | source)
XLA Modules:
  0.0 41.2 jit_solution(6092279366530399659)
XLA Ops:
  0.6 39.9 %shard_map.149 = (bf16[64,128]{1,0:T(8,128)(2,1)S(1)}, bf16[16,64]{1,0:T(8,128)(2,1)S(1)}) custom-call(bf16[4,2048,512]{2,1,0:T(8,128)(2,1)} %v_hbm.1, bf16[4,64,2048]{2,1,0:T(8,128)(2,1)} %bitcast.8, s32[4,4]{1,0:T(4,128)} %tiles_hbm.1, bf16[128,512]{1,0:T(8,128)(2,1)} %dm_hbm.1, f32[4,2048]{1,0:T(4,128)} %gw_hbm.1, s32[4,2048]{1,0:T(4,128)} %ids_hbm.1, ...), custom_call_target="tpu_custom_call" | custom-call | tf_op jit(solution)/shard_map/pallas_call | solution.py:367
  40.5 0.6 %shard_map.150 = (bf16[64,128]{1,0:T(8,128)(2,1)}, bf16[16,64]{1,0:T(8,128)(2,1)}) custom-call(bf16[64,128]{1,0:T(8,128)(2,1)S(1)} %get-tuple-element.6.pot, bf16[16,64]{1,0:T(8,128)(2,1)S(1)} %get-tuple-element.7.cf), custom_call_target="tpu_custom_call" | custom-call | tf_op jit(solution)/shard_map/pallas_call | solution.py:418

commit v4 on v3

--- a/solution.py
+++ b/solution.py
@@ -104,7 +104,6 @@
         return jnp.sum(q * vt[b][at, which].astype(F32), axis=0, keepdims=True)
 
     def prepare(b):
-        pltpu.make_async_copy(vbuf[b], vbuf[b], vsem.at[b]).wait()
         held = [tiles[b, j] for j in range(per_batch)]
 
         def find(t, value, otherwise):
@@ -147,12 +146,12 @@
         if b == 1:
             small[1].wait()
             small[2].wait()
+        pltpu.make_async_copy(vbuf[b], vbuf[b], vsem.at[b]).wait()
         if b:
             dens[b - 1] = part(b - 1, m)
             mask(b - 1)
         prepare(b)
-        if b == batches - 2:
-            passing = receive(0)
+    passing = receive(0)
     for c in small[3:]:
         c.wait()
     pltpu.make_async_copy(w13, w13, msem.at[0]).wait()
@@ -255,8 +254,8 @@
                 acc[q, first + i] = r[(2 * i + q) * slab:(2 * i + q + 1) * slab]
 
     stages = [
-        (0, [(spot(0, i), 1) for i in range(mid)] + [(spot(1, i), 0) for i in range(mid)]),
-        (2 * mid, [(spot(0, i), 0) for i in range(mid)]),
+        (0, [(spot(0, i), 0) for i in range(mid)]),
+        (mid, [(spot(1, i), 0) for i in range(mid)] + [(spot(0, i), 1) for i in range(mid)]),
         (3 * mid, [(spot(1, i), 1) for i in range(mid)]),
     ]
 
@@ -288,18 +287,18 @@
 
 
     def turn(n, carry):
-        keep(quarter(n // 2, jnp.where(n == 1, 0, 1)), jnp.where(n == 0, 0, (n + 1) * mid))
+        keep(quarter(n // 2, (n + 1) // 2), jnp.where(n == 0, 0, (n + 1) * mid))
 
         @pl.when(n == 0)
         def _():
-            across = jnp.concatenate([acc[q, i] for i in range(mid) for q in range(2)], axis=0)
-            keep(across.T, mid)
             give(0)
 
         @pl.when(n == 1)
         def _():
+            across = jnp.concatenate([acc[q, 2 * mid + i] for i in range(mid) for q in range(2)], axis=0)
+            keep(across.T, mid)
+            give(1)
             spread(0)
-            give(1)
 
         @pl.when(n == 2)
         def _():
@@ -310,9 +309,7 @@
 
     lax.fori_loop(0, 3, turn, 0)
     spread(2)
-    early = lax.rem(chip + chip // 2 + 1, 2)
-    for n in range(2):
-        u = early if n == 0 else 1 - early
+    for u in range(2):
         mine = whole[chip, u]
         remote(rin.at[u], rin.at[u], rp_s, rp_r.at[u], pts=buddy).wait_recv()
         for k in range(pairs - 1):

time: 41.3 us -> 40.3 us (0.976)
  Pallas kernels: 40.5 us -> 39.3 us
    pallas_call x1, Pallas kernels: 39.9 us -> 38.7 us  [shards(): pl.pallas_call(functools.partial(kernel, nm, npts, factor), out_shape=(pl...]
where the time goes in v4:
time: 40.3 us; the launch traced here: 40 us
  Pallas kernels  39.3 us (98%)
  between operations  0.64 us (2%)
    pallas_call x1, Pallas kernels, shards(): pl.pallas_call(functools.partial(kernel, nm, npts, factor), out_shape=(pl...  38.7 us

profile of v4, /device:TPU:0, one launch (start us, length us, event | category | flops | bytes accessed | tf_op | source)
XLA Modules:
  0.0 40.0 jit_solution(84474366588063598)
XLA Ops:
  0.6 38.7 %shard_map.149 = (bf16[64,128]{1,0:T(8,128)(2,1)S(1)}, bf16[16,64]{1,0:T(8,128)(2,1)S(1)}) custom-call(bf16[4,2048,512]{2,1,0:T(8,128)(2,1)} %v_hbm.1, bf16[4,64,2048]{2,1,0:T(8,128)(2,1)} %bitcast.8, s32[4,4]{1,0:T(4,128)} %tiles_hbm.1, bf16[128,512]{1,0:T(8,128)(2,1)} %dm_hbm.1, f32[4,2048]{1,0:T(4,128)} %gw_hbm.1, s32[4,2048]{1,0:T(4,128)} %ids_hbm.1, ...), custom_call_target="tpu_custom_call" | custom-call | tf_op jit(solution)/shard_map/pallas_call | solution.py:364
  39.3 0.6 %shard_map.150 = (bf16[64,128]{1,0:T(8,128)(2,1)}, bf16[16,64]{1,0:T(8,128)(2,1)}) custom-call(bf16[64,128]{1,0:T(8,128)(2,1)S(1)} %get-tuple-element.6.pot, bf16[16,64]{1,0:T(8,128)(2,1)S(1)} %get-tuple-element.7.cf), custom_call_target="tpu_custom_call" | custom-call | tf_op jit(solution)/shard_map/pallas_call | solution.py:415

commit v5 on v4

--- a/solution.py
+++ b/solution.py
@@ -33,7 +33,7 @@
     v_hbm, d_hbm, tiles_hbm, dm_hbm, gw_hbm, ids_hbm, scale_hbm, gain_hbm,
     w1_hbm, b1_hbm, w2_hbm, b2_hbm, w3_hbm, b3_hbm,
     out_pot, out_cf,
-    tiles, gw, ids, w13, b12, sgb, w2,
+    tiles, gw, ids, w13, b12, sgb, w2, gain_col, b3_col,
     vbuf, dbuf, vt, oh, dens, pps, panel, cpart, cs_src, cs_in, cz_src, cz_in,
     full, cf_s, cft, acc, psnd, pin, whole, snd, rin, red, zsnd, zin,
     isem, msem, vsem, ag_s, ag_r, fw_s, fw_r, cs_s, cs_r, cz_s, cz_r, cg_s, cg_r, pr_s, pr_r, rp_s, rp_r, rz_s, rz_r,
@@ -62,10 +62,10 @@
         return pltpu.make_async_copy(v_hbm.at[b, :, pl.ds(j * tile, tile)], vbuf[b].at[j], vsem.at[b])
 
     barrier = pltpu.get_barrier_semaphore()
+    for k in range(1, nm):
+        pl.semaphore_signal(barrier, inc=1, device_id={"mat": lax.rem(m + k, nm)}, device_id_type=MESH)
     for k in range(1, npts):
         pl.semaphore_signal(barrier, inc=1, device_id={"pts": lax.rem(p + k, npts)}, device_id_type=MESH)
-    for k in range(1, nm):
-        pl.semaphore_signal(barrier, inc=1, device_id={"mat": lax.rem(m + k, nm)}, device_id_type=MESH)
     for c in small[:3]:
         c.start()
     for j in range(per_batch):
@@ -100,8 +100,8 @@
 
     def part(b, owner, which=slice(None)):
         at = pl.ds(pl.multiple_of(owner * rows, rows), rows)
-        q = jnp.dot(panel[at, :], vt[b][:, which], preferred_element_type=F32)
-        return jnp.sum(q * vt[b][at, which].astype(F32), axis=0, keepdims=True)
+        q = jnp.dot(panel[at, :], vt.at[b][:, which], preferred_element_type=F32)
+        return jnp.sum(q * vt.at[b][at, which].astype(F32), axis=0, keepdims=True)
 
     def prepare(b):
         held = [tiles[b, j] for j in range(per_batch)]
@@ -117,7 +117,7 @@
             x = vbuf[b][spot[t]]
             if ntile != per_batch:
                 x = jnp.where(here[t] == 1, x, jnp.zeros_like(x))
-            vt[b][t * tile:(t + 1) * tile, :] = x.T
+            vt.at[b][t * tile:(t + 1) * tile, :] = x.T
 
     def mask(b):
         which = lax.broadcasted_iota(jnp.int32, (ncent, points), 0)
@@ -161,7 +161,12 @@
     w1, w3 = w13.at[0], w13.at[1]
     b1, b2 = b12.at[0], b12.at[1]
 
-    scale_col = jnp.broadcast_to(scale[...], (128, feat)).T[:, :1]
+    def column(row):
+        return jnp.broadcast_to(row[...], (128, feat)).T[:, :1]
+
+    scale_col = column(scale)
+    gain_col[...] = jnp.broadcast_to(column(gain), gain_col.shape)
+    b3_col[...] = jnp.broadcast_to(column(b3), b3_col.shape)
     cpart[...] = jnp.zeros_like(cpart)
 
     dens[batches - 1] = part(batches - 1, m)
@@ -170,8 +175,13 @@
         for c in passing:
             c.wait_recv()
         passing = receive(k + 1)
-        for b in range(batches):
-            dens[b] += part(b, order[k])
+
+        def step(i, carry):
+            for b in (2 * i, 2 * i + 1):
+                dens[b] += part(b, order[k])
+            return carry
+
+        lax.fori_loop(0, batches // 2, step, 0)
     for c in passing:
         c.wait_recv()
     for b in range(batches):
@@ -212,16 +222,12 @@
     all_cg = remote(others, others, cg_s, cg_r, pts=lax.rem(p + 1, npts))
     all_cg.wait_recv()
 
-    summed = jnp.concatenate([full[lax.rem(p - i - 1 + npts, npts)] for i in range(npts)], axis=0).T
-    inverse = lax.rsqrt(jnp.mean(summed * summed, axis=1, keepdims=True) + 1e-05)
-    normed = (summed * inverse * gain[...]).astype(BF16)
+    summed = jnp.concatenate([full[lax.rem(p - i - 1 + npts, npts)] for i in range(npts)], axis=0)
+    inverse = lax.rsqrt(jnp.mean(summed * summed, axis=0, keepdims=True) + 1e-05)
+    normed = (summed * inverse * gain_col[...]).T.astype(BF16)
     one = silu(jnp.dot(normed, w1[...], preferred_element_type=F32) + b1[...]).astype(BF16)
     two = silu(jnp.dot(one, w2[...], preferred_element_type=F32) + b2[...]).astype(BF16)
-    cf = (lax.dot_general(two, w3[...], NT_DIMS, preferred_element_type=F32) + b3[...]).astype(BF16).astype(F32)
-    cf_s[...] = cf
-    cft[...] = cf.T.astype(BF16)
-    cent = out_cf.shape[0]
-    out_cf[...] = cf_s[pl.ds(pl.multiple_of(p * cent, cent), cent), :].astype(BF16)
+    cft[...] = (lax.dot_general(w3[...], two, NT_DIMS, preferred_element_type=F32) + b3_col[...]).astype(BF16)
 
     def spot(u, i):
         return 2 * i + (i + u) % 2 if isinstance(u, int) else 2 * i + lax.rem(i + u, 2)
@@ -239,7 +245,7 @@
 
     def side(b, u):
         return jnp.concatenate([
-            vt[b][pl.ds(pl.multiple_of(spot(u, i) * tile, tile), tile), :] for i in range(mid)], axis=0)
+            vt.at[b][pl.ds(pl.multiple_of(spot(u, i) * tile, tile), tile), :] for i in range(mid)], axis=0)
 
     def quarter(u, w):
         r = 0
@@ -308,6 +314,9 @@
         return carry
 
     lax.fori_loop(0, 3, turn, 0)
+    cf_s[...] = cft[...].astype(F32).T
+    cent = out_cf.shape[0]
+    out_cf[...] = cf_s[pl.ds(pl.multiple_of(p * cent, cent), cent), :].astype(BF16)
     spread(2)
     for u in range(2):
         mine = whole[chip, u]
@@ -374,9 +383,11 @@
             pltpu.VMEM((2, 1, hid), F32),
             pltpu.VMEM((3, 1, feat), F32),
             pltpu.VMEM((hid, hid), BF16),
+            pltpu.VMEM((feat, ncent), F32),
+            pltpu.VMEM((feat, ncent), F32),
             [pltpu.VMEM((per_batch, points, tile), BF16) for _ in range(batches)],
             pltpu.VMEM((batches, feat, points), BF16),
-            [pltpu.VMEM((nb, points), BF16) for _ in range(batches)],
+            pltpu.VMEM((batches, nb, points), BF16),
             pltpu.VMEM((batches, ncent, points), BF16),
             pltpu.VMEM((batches, 1, points), F32),
             pltpu.VMEM((batches, 1, points), F32),

time: 40.3 us -> 40.3 us (level)
  no operation moved by 1% of the time
where the time goes in v5:
time: 40.3 us; the launch traced here: 39.9 us
  Pallas kernels  39.3 us (98%)
  between operations  0.64 us (2%)
    pallas_call x1, Pallas kernels, shards(): pl.pallas_call(functools.partial(kernel, nm, npts, factor), out_shape=(pl...  38.6 us

profile of v5, /device:TPU:0, one launch (start us, length us, event | category | flops | bytes accessed | tf_op | source)
XLA Modules:
  0.0 39.9 jit_solution(7839362826410783166)
XLA Ops:
  0.6 38.6 %shard_map.149 = (bf16[64,128]{1,0:T(8,128)(2,1)S(1)}, bf16[16,64]{1,0:T(8,128)(2,1)S(1)}) custom-call(bf16[4,2048,512]{2,1,0:T(8,128)(2,1)} %v_hbm.1, bf16[4,64,2048]{2,1,0:T(8,128)(2,1)} %bitcast.8, s32[4,4]{1,0:T(4,128)} %tiles_hbm.1, bf16[128,512]{1,0:T(8,128)(2,1)} %dm_hbm.1, f32[4,2048]{1,0:T(4,128)} %gw_hbm.1, s32[4,2048]{1,0:T(4,128)} %ids_hbm.1, ...), custom_call_target="tpu_custom_call" | custom-call | tf_op jit(solution)/shard_map/pallas_call | solution.py:373
  39.3 0.6 %shard_map.150 = (bf16[64,128]{1,0:T(8,128)(2,1)}, bf16[16,64]{1,0:T(8,128)(2,1)}) custom-call(bf16[64,128]{1,0:T(8,128)(2,1)S(1)} %get-tuple-element.6.pot, bf16[16,64]{1,0:T(8,128)(2,1)S(1)} %get-tuple-element.7.cf), custom_call_target="tpu_custom_call" | custom-call | tf_op jit(solution)/shard_map/pallas_call | solution.py:426

commit v6 on v5

--- a/solution.py
+++ b/solution.py
@@ -36,7 +36,7 @@
     tiles, gw, ids, w13, b12, sgb, w2, gain_col, b3_col,
     vbuf, dbuf, vt, oh, dens, pps, panel, cpart, cs_src, cs_in, cz_src, cz_in,
     full, cf_s, cft, acc, psnd, pin, whole, snd, rin, red, zsnd, zin,
-    isem, msem, vsem, ag_s, ag_r, fw_s, fw_r, cs_s, cs_r, cz_s, cz_r, cg_s, cg_r, pr_s, pr_r, rp_s, rp_r, rz_s, rz_r,
+    isem, msem, vsem, ag_s, ag_r, fw_r, cs_s, cs_r, cz_s, cz_r, cg_s, cg_r, pr_r, rp_r, rz_s, rz_r,
 ):
     m = lax.axis_index("mat")
     p = lax.axis_index("pts")
@@ -136,7 +136,7 @@
         mine = []
         for h in range(1, SPLIT):
             i = k * (SPLIT - 1) + h - 1
-            c = remote(held, held, fw_s, fw_r.at[i], pts=base + lax.rem(g + h, SPLIT))
+            c = remote(held, held, ag_s, fw_r.at[i], pts=base + lax.rem(g + h, SPLIT))
             c.start()
             mine.append(c)
         fw.extend(mine)
@@ -268,7 +268,7 @@
     def pair(n):
         first, entries = stages[n]
         at = pl.ds(first, len(entries))
-        return remote(psnd.at[at], pin.at[at], pr_s, pr_r.at[n], pts=buddy)
+        return remote(psnd.at[at], pin.at[at], ag_s, pr_r.at[n], pts=buddy)
 
     def give(n):
         first, entries = stages[n]
@@ -277,7 +277,7 @@
         pair(n).start()
 
     def plane(to, u):
-        return remote(snd.at[to, u], rin.at[u, lax.rem(to - chip - 1 + pairs, pairs)], rp_s, rp_r.at[u], pts=2 * to + core)
+        return remote(snd.at[to, u], rin.at[u, lax.rem(to - chip - 1 + pairs, pairs)], ag_s, rp_r.at[u], pts=2 * to + core)
 
     def spread(n):
         first, entries = stages[n]
@@ -320,7 +320,7 @@
     spread(2)
     for u in range(2):
         mine = whole[chip, u]
-        remote(rin.at[u], rin.at[u], rp_s, rp_r.at[u], pts=buddy).wait_recv()
+        remote(rin.at[u], rin.at[u], ag_s, rp_r.at[u], pts=buddy).wait_recv()
         for k in range(pairs - 1):
             mine = mine + rin[u, k].astype(F32)
         for i in range(mid):
@@ -340,12 +340,9 @@
 
     for c in (all_cs, all_cz, all_cg, all_rz):
         c.wait_send()
-    sent = panel.at[pl.ds(0, (nm - 1) * piece)]
-    remote(sent, sent, ag_s, ag_r.at[m], mat=lax.rem(m + 1, nm)).wait_send()
-    sent = panel.at[pl.ds(0, (nm - 1) * (SPLIT - 1) * piece)]
-    remote(sent, sent, fw_s, fw_r.at[0], pts=buddy).wait_send()
-    remote(psnd, pin, pr_s, pr_r.at[0], pts=buddy).wait_send()
-    remote(rin, rin, rp_s, rp_r.at[0], pts=buddy).wait_send()
+    moved = (nm - 1) * SPLIT * piece * nb + (npts + 2 * (pairs - 1)) * slab * (nb // 2)
+    sent = vt.at[0, pl.ds(0, moved // points)]
+    remote(sent, sent, ag_s, ag_r.at[m], pts=buddy).wait_send()
 
 
 def shards(
@@ -410,9 +407,9 @@
             pltpu.VMEM((nm, slab, width), BF16),
             pltpu.VMEM((nm - 1, slab, width), BF16),
             dma((6,)), dma((3,)), dma((batches,)),
-            dma, dma((nm,)), dma, dma((nfw,)),
+            dma, dma((nm,)), dma((nfw,)),
             dma, dma, dma, dma, dma, dma,
-            dma, dma((3,)), dma, dma((2,)), dma, dma,
+            dma((3,)), dma((2,)), dma, dma,
         ],
         compiler_params=pltpu.CompilerParams(
             collective_id=0, has_side_effects=True, vmem_limit_bytes=60 * 1024 * 1024

time: 40.3 us -> 40.3 us (level)
  no operation moved by 1% of the time
where the time goes in v6:
time: 40.3 us; the launch traced here: 39.9 us
  Pallas kernels  39.2 us (97%)
  between operations  0.64 us (2%)
    pallas_call x1, Pallas kernels, shards(): pl.pallas_call(functools.partial(kernel, nm, npts, factor), out_shape=(pl...  38.6 us

profile of v6, /device:TPU:0, one launch (start us, length us, event | category | flops | bytes accessed | tf_op | source)
XLA Modules:
  0.0 39.9 jit_solution(12543422255535575359)
XLA Ops:
  0.6 38.6 %shard_map.149 = (bf16[64,128]{1,0:T(8,128)(2,1)S(1)}, bf16[16,64]{1,0:T(8,128)(2,1)S(1)}) custom-call(bf16[4,2048,512]{2,1,0:T(8,128)(2,1)} %v_hbm.1, bf16[4,64,2048]{2,1,0:T(8,128)(2,1)} %bitcast.8, s32[4,4]{1,0:T(4,128)} %tiles_hbm.1, bf16[128,512]{1,0:T(8,128)(2,1)} %dm_hbm.1, f32[4,2048]{1,0:T(4,128)} %gw_hbm.1, s32[4,2048]{1,0:T(4,128)} %ids_hbm.1, ...), custom_call_target="tpu_custom_call" | custom-call | tf_op jit(solution)/shard_map/pallas_call | solution.py:370
  39.2 0.6 %shard_map.150 = (bf16[64,128]{1,0:T(8,128)(2,1)}, bf16[16,64]{1,0:T(8,128)(2,1)}) custom-call(bf16[64,128]{1,0:T(8,128)(2,1)S(1)} %get-tuple-element.6.pot, bf16[16,64]{1,0:T(8,128)(2,1)S(1)} %get-tuple-element.7.cf), custom_call_target="tpu_custom_call" | custom-call | tf_op jit(solution)/shard_map/pallas_call | solution.py:423
